TPU v7x, 512 devices: a whole 4x8x8 slice. The times are simulated.
512 devices in a mesh: row: 16 (over z, core), col: 32 (over y, x).
Axes of the slice: x: 4, y: 8, z: 8, core: 2. Of those that a mesh axis runs over, the one named last changes fastest.
Arguments:
- embeddings: bfloat16 [2048, 512], P('row'), may hold values from -6 to 6
- row_weight: bfloat16 [512, 32], replicated, may hold values from -0.25 to 0.25
- col_weight: bfloat16 [512, 32], replicated, may hold values from -0.25 to 0.25
- conv_weights: bfloat16 [3, 32, 32, 3, 3], replicated, may hold values from -0.5 to 0.5
- conv_bias: float32 [3, 32], replicated, may hold values from -3 to 3
- head_weight: bfloat16 [32], replicated, may hold values from -1 to 1
Outputs:
- contact_map: float32 [2048, 2048], P('row', 'col')
All inputs are finite; a program needn't handle non-finite values.
Results may differ from a plain program's by a relative error of at most 0.023.
Values may be sent and summed in bfloat16 or wider, within the bound.
A program may use at most 64 MiB of HBM per device.

v0:
```python
import jax
import jax.numpy as jnp
from jax import lax
from jax.sharding import PartitionSpec as P


def spread(value, axis, source):
    kept = jnp.where(lax.axis_index(axis) == source, value, 0).astype(value.dtype)
    return lax.psum(kept, axis)


def extended(cells, sides, width):
    for axis, dim in sides:
        count = lax.axis_size(axis)
        ends = count - 1
        head = lax.slice_in_dim(cells, 0, width, axis=dim)
        tail = lax.slice_in_dim(cells, cells.shape[dim] - width, cells.shape[dim], axis=dim)
        cells = jnp.concatenate(
            [
                lax.ppermute(tail, axis, [(i, (i + 1) % count) for i in range(ends)]),
                cells,
                lax.ppermute(head, axis, [((i + 1) % count, i) for i in range(ends)]),
            ],
            axis=dim,
        )
    return cells


def dilated_level(padded, weight, level_bias, dilation):
    summed = lax.conv_general_dilated(
        padded[None],
        weight,
        (1, 1),
        "VALID",
        rhs_dilation=(dilation, dilation),
        dimension_numbers=("NCHW", "OIHW", "NCHW"),
        preferred_element_type=jnp.float32,
    )[0]
    return jax.nn.relu(summed + level_bias[:, None, None]).astype(jnp.bfloat16)


def pair_tile(rows_part, cols_part):
    return (
        rows_part.T.astype(jnp.float32)[:, :, None] + cols_part.T.astype(jnp.float32)[:, None, :]
    ).astype(jnp.bfloat16)


def body(embeddings, row_weight, col_weight, conv_weights, conv_bias, head_weight):
    row_bins = embeddings.shape[0]
    total_bins = row_bins * lax.axis_size("row")
    col_bins = total_bins // lax.axis_size("col")
    first_col = lax.axis_index("col") * col_bins
    owner_row = first_col // row_bins
    offset = first_col - owner_row * row_bins
    dilations = (1, 2, 4)
    row_feats = jnp.dot(embeddings, row_weight, preferred_element_type=jnp.float32).astype(
        jnp.bfloat16
    )
    owner_block = spread(embeddings, "row", owner_row)
    col_rows = lax.dynamic_slice_in_dim(owner_block, offset, col_bins, 0)
    col_feats = jnp.dot(col_rows, col_weight, preferred_element_type=jnp.float32).astype(
        jnp.bfloat16
    )
    current = pair_tile(row_feats, col_feats)
    for level_number, dilation in enumerate(dilations):
        padded = extended(current, (("row", 1), ("col", 2)), dilation)
        current = dilated_level(
            padded, conv_weights[level_number], conv_bias[level_number], dilation
        )
    return jnp.einsum("c,crj->rj", head_weight, current, preferred_element_type=jnp.float32)


def solution(mesh):
    return jax.shard_map(
        body,
        mesh=mesh,
        in_specs=(P("row", None), P(), P(), P(), P(), P()),
        out_specs=P("row", "col"),
        check_vma=False,
    )
```

profile of v0, /device:TPU:223, one launch (start us, length us, event | category | flops | bytes accessed | tf_op | source)
XLA Modules:
  0.0 261.4 jit_solution(6402877888625267361)
XLA Ops:
  6.5 1.6 broadcast_select_fusion.3
  8.2 1.0 fusion.35
  9.2 117.9 %all-reduce.2.cloned.1.call-done = bf16[128,512]{1,0:T(8,128)(2,1)} async-done(((bf16[128,512]{1,0:T(8,128)(2,1)}), bf16[128,512]{1,0:T(8,128)(2,1)}) %all-reduce.2.cloned.1.call-update) | async-done | bytes 131088 | tf_op jit(solution)/shard_map/psum | solution.py:9
  127.1 1.0 fusion.34
  128.2 0.3 add_convert_fusion
  128.5 0.2 fusion.68
  128.7 4.1 %collective-permute-start = (bf16[32,1,64]{1,0,2:T(8,128)(2,1)S(1)}, bf16[32,1,64]{1,0,2:T(8,128)(2,1)S(1)}, u32[]{:S(2)}, u32[]{:S(2)}) collective-permute-start(bf16[32,1,64]{1,0,2:T(8,128)(2,1)S(1)} %get-tuple-element.15), channel_id=1, source_target_pairs={{0,32},{32,64},{64,96},{96,128},{128,160},{160,192},{192,224},{224... | collective-permute-start | bytes 12296 | tf_op jit(solution)/shard_map/ppermute | solution.py:20
  132.8 1.9 collective-permute-start.1
  134.8 4.2 %collective-permute-done = bf16[32,1,64]{1,0,2:T(8,128)(2,1)S(1)} collective-permute-done((bf16[32,1,64]{1,0,2:T(8,128)(2,1)S(1)}, bf16[32,1,64]{1,0,2:T(8,128)(2,1)S(1)}, u32[]{:S(2)}, u32[]{:S(2)}) %collective-permute-start) | collective-permute-done | bytes 4128 | tf_op jit(solution)/shard_map/ppermute | solution.py:20
  138.9 5.6 %collective-permute-done.1 = bf16[32,1,64]{1,0,2:T(8,128)(2,1)S(1)} collective-permute-done((bf16[32,1,64]{1,0,2:T(8,128)(2,1)S(1)}, bf16[32,1,64]{1,0,2:T(8,128)(2,1)S(1)}, u32[]{:S(2)}, u32[]{:S(2)}) %collective-permute-start.1) | collective-permute-done | bytes 4128 | tf_op jit(solution)/shard_map/ppermute | solution.py:22
  144.6 4.3 %collective-permute-start.2 = (bf16[32,130,1]{1,0,2:T(8,128)(2,1)S(1)}, bf16[32,130,1]{1,0,2:T(8,128)(2,1)S(1)}, u32[]{:S(2)}, u32[]{:S(2)}) collective-permute-start(bf16[32,130,1]{1,0,2:T(8,128)(2,1)S(1)} %get-tuple-element.9), channel_id=1, source_target_pairs={{0,1},{1,2},{2,3},{3,4},{4,5},{5,6},{6,7},{7,8},{8,9},{9,10},{10,1... | collective-permute-start | bytes 24968 | tf_op jit(solution)/shard_map/ppermute | solution.py:20
  149.0 1.9 collective-permute-start.3
  150.9 5.8 %collective-permute-done.3 = bf16[32,130,1]{1,0,2:T(8,128)(2,1)S(1)} collective-permute-done((bf16[32,130,1]{1,0,2:T(8,128)(2,1)S(1)}, bf16[32,130,1]{1,0,2:T(8,128)(2,1)S(1)}, u32[]{:S(2)}, u32[]{:S(2)}) %collective-permute-start.3) | collective-permute-done | bytes 8352 | tf_op jit(solution)/shard_map/ppermute | solution.py:22
  156.8 0.7 maximum_bitcast_fusion.1
  157.4 0.3 pad
  157.8 3.1 %copy.32 = bf16[32,130,1,8,9]{0,3,4,1,2:T(8,128)(2,1)} copy(bf16[32,130,1,8,9]{1,0,4,3,2:T(8,128)(2,1)S(1)} %bitcast.84) | data formatting | bytes 1198080 | tf_op jit(solution)/shard_map/conv_general_dilated | solution.py:30
  160.8 1.2 slice.80
  162.1 6.6 %broadcast_select_fusion.2 = f32[128,8,9,32]{3,1,2,0:T(8,128)} fusion(pred[8,9]{0,1:T(8,128)(4,1)S(1)} %copy-done.4, bf16[32,130,1,7,2]{0,3,4,1,2:T(8,128)(2,1)S(1)} %slice.80, bf16[32,130,1,8,9]{0,3,4,1,2:T(8,128)(2,1)} %copy.32, bf16[3,32,32,3,3]{2,1,4,3,0:T(8,128)(2,1)S(1)} %copy-done.3), kind=kOutput, calls=%fused_computation.27 | convolution fusion | flops 172360704 | bytes 2386944 | tf_op jit(solution)/shard_map/conv_general_dilated | solution.py:30
  168.6 3.7 %copy.33 = f32[128,8,9,32]{0,3,2,1:T(8,128)S(1)} copy(f32[128,8,9,32]{3,1,2,0:T(8,128)} %broadcast_select_fusion.2) | data formatting | bytes 2359296 | tf_op jit(solution)/shard_map/conv_general_dilated | solution.py:30
  172.4 0.2 fusion.44
  172.6 0.2 fusion.67
  172.8 3.2 %collective-permute-start.4 = (bf16[32,2,64]{1,0,2:T(8,128)(2,1)S(1)}, bf16[32,2,64]{1,0,2:T(8,128)(2,1)S(1)}, u32[]{:S(2)}, u32[]{:S(2)}) collective-permute-start(bf16[32,2,64]{1,0,2:T(8,128)(2,1)S(1)} %get-tuple-element.13), channel_id=1, source_target_pairs={{0,32},{32,64},{64,96},{96,128},{128,160},{160,192},{192,224},{224... | collective-permute-start | bytes 24584 | tf_op jit(solution)/shard_map/ppermute | solution.py:20
  176.0 1.9 collective-permute-start.5
  177.9 4.2 %collective-permute-done.4 = bf16[32,2,64]{1,0,2:T(8,128)(2,1)S(1)} collective-permute-done((bf16[32,2,64]{1,0,2:T(8,128)(2,1)S(1)}, bf16[32,2,64]{1,0,2:T(8,128)(2,1)S(1)}, u32[]{:S(2)}, u32[]{:S(2)}) %collective-permute-start.4) | collective-permute-done | bytes 8224 | tf_op jit(solution)/shard_map/ppermute | solution.py:20
  182.1 5.6 %collective-permute-done.5 = bf16[32,2,64]{1,0,2:T(8,128)(2,1)S(1)} collective-permute-done((bf16[32,2,64]{1,0,2:T(8,128)(2,1)S(1)}, bf16[32,2,64]{1,0,2:T(8,128)(2,1)S(1)}, u32[]{:S(2)}, u32[]{:S(2)}) %collective-permute-start.5) | collective-permute-done | bytes 8224 | tf_op jit(solution)/shard_map/ppermute | solution.py:22
  187.8 1.9 collective-permute-start.6
  189.7 3.4 %collective-permute-start.7 = (bf16[32,132,2]{1,0,2:T(8,128)(2,1)S(1)}, bf16[32,132,2]{1,0,2:T(8,128)(2,1)S(1)}, u32[]{:S(2)}, u32[]{:S(2)}) collective-permute-start(bf16[32,132,2]{1,0,2:T(8,128)(2,1)S(1)} %get-tuple-element.8), channel_id=1, source_target_pairs={{1,0},{2,1},{3,2},{4,3},{5,4},{6,5},{7,6},{8,7},{9,8},{10,9},{11,1... | collective-permute-start | bytes 50696 | tf_op jit(solution)/shard_map/ppermute | solution.py:22
  193.1 4.6 %collective-permute-done.7 = bf16[32,132,2]{1,0,2:T(8,128)(2,1)S(1)} collective-permute-done((bf16[32,132,2]{1,0,2:T(8,128)(2,1)S(1)}, bf16[32,132,2]{1,0,2:T(8,128)(2,1)S(1)}, u32[]{:S(2)}, u32[]{:S(2)}) %collective-permute-start.7) | collective-permute-done | bytes 16928 | tf_op jit(solution)/shard_map/ppermute | solution.py:22
  197.7 0.6 maximum_bitcast_fusion
  198.3 1.3 pad.2
  199.6 3.3 %copy.35 = bf16[32,132,1,8,9]{0,3,4,1,2:T(8,128)(2,1)S(1)} copy(bf16[32,132,1,8,9]{1,0,4,3,2:T(8,128)(2,1)} %bitcast.82) | data formatting | bytes 1216512 | tf_op jit(solution)/shard_map/conv_general_dilated | solution.py:30
  202.9 0.3 slice.84
  203.2 5.5 %broadcast_select_fusion.1 = f32[128,8,9,32]{3,1,2,0:T(8,128)} fusion(pred[8,9]{0,1:T(8,128)(4,1)S(1)} %copy-done.4, bf16[32,132,1,7,4]{0,3,4,1,2:T(8,128)(2,1)S(1)} %slice.84, bf16[32,132,1,8,9]{0,3,4,1,2:T(8,128)(2,1)S(1)} %copy.35, bf16[3,32,32,3,3]{2,1,4,3,0:T(8,128)(2,1)S(1)} %copy-done.3), kind=kOutput, calls=%fused_computation.26 | convolution fusion | flops 172800000 | bytes 4769792 | tf_op jit(solution)/shard_map/conv_general_dilated | solution.py:30
  208.7 3.7 %copy.36 = f32[128,8,9,32]{0,3,2,1:T(8,128)S(1)} copy(f32[128,8,9,32]{3,1,2,0:T(8,128)} %broadcast_select_fusion.1) | data formatting | bytes 2359296 | tf_op jit(solution)/shard_map/conv_general_dilated | solution.py:30
  212.6 0.2 fusion.66
  212.8 2.9 %collective-permute-start.8 = (bf16[32,4,64]{1,0,2:T(8,128)(2,1)S(1)}, bf16[32,4,64]{1,0,2:T(8,128)(2,1)S(1)}, u32[]{:S(2)}, u32[]{:S(2)}) collective-permute-start(bf16[32,4,64]{1,0,2:T(8,128)(2,1)S(1)} %get-tuple-element.11), channel_id=1, source_target_pairs={{0,32},{32,64},{64,96},{96,128},{128,160},{160,192},{192,224},{224... | collective-permute-start | bytes 49160 | tf_op jit(solution)/shard_map/ppermute | solution.py:20
  215.7 1.9 collective-permute-start.9
  217.7 4.2 %collective-permute-done.8 = bf16[32,4,64]{1,0,2:T(8,128)(2,1)S(1)} collective-permute-done((bf16[32,4,64]{1,0,2:T(8,128)(2,1)S(1)}, bf16[32,4,64]{1,0,2:T(8,128)(2,1)S(1)}, u32[]{:S(2)}, u32[]{:S(2)}) %collective-permute-start.8) | collective-permute-done | bytes 16416 | tf_op jit(solution)/shard_map/ppermute | solution.py:20
  221.9 5.6 %collective-permute-done.9 = bf16[32,4,64]{1,0,2:T(8,128)(2,1)S(1)} collective-permute-done((bf16[32,4,64]{1,0,2:T(8,128)(2,1)S(1)}, bf16[32,4,64]{1,0,2:T(8,128)(2,1)S(1)}, u32[]{:S(2)}, u32[]{:S(2)}) %collective-permute-start.9) | collective-permute-done | bytes 16416 | tf_op jit(solution)/shard_map/ppermute | solution.py:22
  227.6 1.9 collective-permute-start.10
  229.5 3.5 %collective-permute-start.11 = (bf16[32,136,4]{1,0,2:T(8,128)(2,1)S(1)}, bf16[32,136,4]{1,0,2:T(8,128)(2,1)S(1)}, u32[]{:S(2)}, u32[]{:S(2)}) collective-permute-start(bf16[32,136,4]{1,0,2:T(8,128)(2,1)S(1)} %get-tuple-element.6), channel_id=1, source_target_pairs={{1,0},{2,1},{3,2},{4,3},{5,4},{6,5},{7,6},{8,7},{9,8},{10,9},{11,1... | collective-permute-start | bytes 104456 | tf_op jit(solution)/shard_map/ppermute | solution.py:22
  233.1 4.8 %collective-permute-done.11 = bf16[32,136,4]{1,0,2:T(8,128)(2,1)S(1)} collective-permute-done((bf16[32,136,4]{1,0,2:T(8,128)(2,1)S(1)}, bf16[32,136,4]{1,0,2:T(8,128)(2,1)S(1)}, u32[]{:S(2)}, u32[]{:S(2)}) %collective-permute-start.11) | collective-permute-done | bytes 34848 | tf_op jit(solution)/shard_map/ppermute | solution.py:22
  237.8 1.6 pad_maximum_fusion
  239.5 3.0 %copy.38 = bf16[32,136,1,8,9]{0,3,4,1,2:T(8,128)(2,1)S(1)} copy(bf16[32,136,1,8,9]{1,0,4,3,2:T(8,128)(2,1)} %bitcast.83) | data formatting | bytes 1253376 | tf_op jit(solution)/shard_map/conv_general_dilated | solution.py:30
  242.5 0.7 slice.88
  243.1 6.7 %broadcast_select_fusion = f32[128,8,9,32]{3,1,2,0:T(8,128)} fusion(pred[8,9]{0,1:T(8,128)(4,1)S(1)} %copy-done.4, bf16[32,136,1,7,8]{0,3,4,1,2:T(8,128)(2,1)S(1)} %slice.88, bf16[32,136,1,8,9]{0,3,4,1,2:T(8,128)(2,1)S(1)} %copy.38, bf16[3,32,32,3,3]{2,1,4,3,0:T(8,128)(2,1)S(1)} %copy-done.3), kind=kOutput, calls=%fused_computation.25 | convolution fusion | flops 173715456 | bytes 5990400 | tf_op jit(solution)/shard_map/conv_general_dilated | solution.py:30
  249.8 3.8 %copy.39 = f32[128,8,9,32]{0,3,2,1:T(8,128)S(1)} copy(f32[128,8,9,32]{3,1,2,0:T(8,128)} %broadcast_select_fusion) | data formatting | bytes 2359296 | tf_op jit(solution)/shard_map/conv_general_dilated | solution.py:30
  253.6 0.9 fusion.45
  (21 shorter events, 0.6 us)
Async XLA Ops:
  6.5 1.6 copy-start
  6.5 120.6 %all-reduce.2.cloned.1.call-start = ((), (), s32[]{:S(2)}) async-start(), calls=%async_computation | async-start | bytes 262144 | tf_op jit(solution)/shard_map/psum | solution.py:9
  8.1 142.8 %copy-start.1 = (f32[3,32]{1,0:T(4,128)S(1)}, f32[3,32]{1,0:T(4,128)}, u32[]{:S(2)}) copy-start(f32[3,32]{1,0:T(4,128)} %param.10) | copy-start | bytes 1156
  128.7 10.2 %collective-permute-start = (bf16[32,1,64]{1,0,2:T(8,128)(2,1)S(1)}, bf16[32,1,64]{1,0,2:T(8,128)(2,1)S(1)}, u32[]{:S(2)}, u32[]{:S(2)}) collective-permute-start(bf16[32,1,64]{1,0,2:T(8,128)(2,1)S(1)} %get-tuple-element.15), channel_id=1, source_target_pairs={{0,32},{32,64},{64,96},{96,128},{128,160},{160,192},{192,224},{224... | collective-permute-start | bytes 12296 | tf_op jit(solution)/shard_map/ppermute | solution.py:20
  132.8 11.7 %collective-permute-start.1 = (bf16[32,1,64]{1,0,2:T(8,128)(2,1)S(1)}, bf16[32,1,64]{1,0,2:T(8,128)(2,1)S(1)}, u32[]{:S(2)}, u32[]{:S(2)}) collective-permute-start(bf16[32,1,64]{1,0,2:T(8,128)(2,1)S(1)} %get-tuple-element.16), channel_id=1, source_target_pairs={{32,0},{64,32},{96,64},{128,96},{160,128},{192,160},{224,192},{256... | collective-permute-start | bytes 12296 | tf_op jit(solution)/shard_map/ppermute | solution.py:22
  144.6 6.3 %collective-permute-start.2 = (bf16[32,130,1]{1,0,2:T(8,128)(2,1)S(1)}, bf16[32,130,1]{1,0,2:T(8,128)(2,1)S(1)}, u32[]{:S(2)}, u32[]{:S(2)}) collective-permute-start(bf16[32,130,1]{1,0,2:T(8,128)(2,1)S(1)} %get-tuple-element.9), channel_id=1, source_target_pairs={{0,1},{1,2},{2,3},{3,4},{4,5},{5,6},{6,7},{7,8},{8,9},{9,10},{10,1... | collective-permute-start | bytes 24968 | tf_op jit(solution)/shard_map/ppermute | solution.py:20
  149.0 7.8 %collective-permute-start.3 = (bf16[32,130,1]{1,0,2:T(8,128)(2,1)S(1)}, bf16[32,130,1]{1,0,2:T(8,128)(2,1)S(1)}, u32[]{:S(2)}, u32[]{:S(2)}) collective-permute-start(bf16[32,130,1]{1,0,2:T(8,128)(2,1)S(1)} %get-tuple-element.10), channel_id=1, source_target_pairs={{1,0},{2,1},{3,2},{4,3},{5,4},{6,5},{7,6},{8,7},{9,8},{10,9},{11,1... | collective-permute-start | bytes 24968 | tf_op jit(solution)/shard_map/ppermute | solution.py:22
  157.7 4.3 %copy-start.3 = (bf16[3,32,32,3,3]{2,1,4,3,0:T(8,128)(2,1)S(1)}, bf16[3,32,32,3,3]{2,1,4,3,0:T(8,128)(2,1)}, u32[]{:S(2)}) copy-start(bf16[3,32,32,3,3]{2,1,4,3,0:T(8,128)(2,1)} %param.9) | copy-start | bytes 165892
  157.8 4.3 %copy-start.4 = (pred[8,9]{0,1:T(8,128)(4,1)S(1)}, pred[8,9]{0,1:T(8,128)(4,1)}, u32[]{:S(2)}) copy-start(pred[8,9]{0,1:T(8,128)(4,1)} %constant.47) | copy-start | bytes 220
  172.8 9.3 %collective-permute-start.4 = (bf16[32,2,64]{1,0,2:T(8,128)(2,1)S(1)}, bf16[32,2,64]{1,0,2:T(8,128)(2,1)S(1)}, u32[]{:S(2)}, u32[]{:S(2)}) collective-permute-start(bf16[32,2,64]{1,0,2:T(8,128)(2,1)S(1)} %get-tuple-element.13), channel_id=1, source_target_pairs={{0,32},{32,64},{64,96},{96,128},{128,160},{160,192},{192,224},{224... | collective-permute-start | bytes 24584 | tf_op jit(solution)/shard_map/ppermute | solution.py:20
  176.0 11.7 %collective-permute-start.5 = (bf16[32,2,64]{1,0,2:T(8,128)(2,1)S(1)}, bf16[32,2,64]{1,0,2:T(8,128)(2,1)S(1)}, u32[]{:S(2)}, u32[]{:S(2)}) collective-permute-start(bf16[32,2,64]{1,0,2:T(8,128)(2,1)S(1)} %get-tuple-element.14), channel_id=1, source_target_pairs={{32,0},{64,32},{96,64},{128,96},{160,128},{192,160},{224,192},{256... | collective-permute-start | bytes 24584 | tf_op jit(solution)/shard_map/ppermute | solution.py:22
  187.8 5.3 %collective-permute-start.6 = (bf16[32,132,2]{1,0,2:T(8,128)(2,1)S(1)}, bf16[32,132,2]{1,0,2:T(8,128)(2,1)S(1)}, u32[]{:S(2)}, u32[]{:S(2)}) collective-permute-start(bf16[32,132,2]{1,0,2:T(8,128)(2,1)S(1)} %get-tuple-element.7), channel_id=1, source_target_pairs={{0,1},{1,2},{2,3},{3,4},{4,5},{5,6},{6,7},{7,8},{8,9},{9,10},{10,1... | collective-permute-start | bytes 50696 | tf_op jit(solution)/shard_map/ppermute | solution.py:20
  189.7 8.0 %collective-permute-start.7 = (bf16[32,132,2]{1,0,2:T(8,128)(2,1)S(1)}, bf16[32,132,2]{1,0,2:T(8,128)(2,1)S(1)}, u32[]{:S(2)}, u32[]{:S(2)}) collective-permute-start(bf16[32,132,2]{1,0,2:T(8,128)(2,1)S(1)} %get-tuple-element.8), channel_id=1, source_target_pairs={{1,0},{2,1},{3,2},{4,3},{5,4},{6,5},{7,6},{8,7},{9,8},{10,9},{11,1... | collective-permute-start | bytes 50696 | tf_op jit(solution)/shard_map/ppermute | solution.py:22
  212.8 9.0 %collective-permute-start.8 = (bf16[32,4,64]{1,0,2:T(8,128)(2,1)S(1)}, bf16[32,4,64]{1,0,2:T(8,128)(2,1)S(1)}, u32[]{:S(2)}, u32[]{:S(2)}) collective-permute-start(bf16[32,4,64]{1,0,2:T(8,128)(2,1)S(1)} %get-tuple-element.11), channel_id=1, source_target_pairs={{0,32},{32,64},{64,96},{96,128},{128,160},{160,192},{192,224},{224... | collective-permute-start | bytes 49160 | tf_op jit(solution)/shard_map/ppermute | solution.py:20
  215.7 11.7 %collective-permute-start.9 = (bf16[32,4,64]{1,0,2:T(8,128)(2,1)S(1)}, bf16[32,4,64]{1,0,2:T(8,128)(2,1)S(1)}, u32[]{:S(2)}, u32[]{:S(2)}) collective-permute-start(bf16[32,4,64]{1,0,2:T(8,128)(2,1)S(1)} %get-tuple-element.12), channel_id=1, source_target_pairs={{32,0},{64,32},{96,64},{128,96},{160,128},{192,160},{224,192},{256... | collective-permute-start | bytes 49160 | tf_op jit(solution)/shard_map/ppermute | solution.py:22
  227.6 5.5 %collective-permute-start.10 = (bf16[32,136,4]{1,0,2:T(8,128)(2,1)S(1)}, bf16[32,136,4]{1,0,2:T(8,128)(2,1)S(1)}, u32[]{:S(2)}, u32[]{:S(2)}) collective-permute-start(bf16[32,136,4]{1,0,2:T(8,128)(2,1)S(1)} %get-tuple-element.5), channel_id=1, source_target_pairs={{0,1},{1,2},{2,3},{3,4},{4,5},{5,6},{6,7},{7,8},{8,9},{9,10},{10,1... | collective-permute-start | bytes 104456 | tf_op jit(solution)/shard_map/ppermute | solution.py:20
  229.5 8.3 %collective-permute-start.11 = (bf16[32,136,4]{1,0,2:T(8,128)(2,1)S(1)}, bf16[32,136,4]{1,0,2:T(8,128)(2,1)S(1)}, u32[]{:S(2)}, u32[]{:S(2)}) collective-permute-start(bf16[32,136,4]{1,0,2:T(8,128)(2,1)S(1)} %get-tuple-element.6), channel_id=1, source_target_pairs={{1,0},{2,1},{3,2},{4,3},{5,4},{6,5},{7,6},{8,7},{9,8},{10,9},{11,1... | collective-permute-start | bytes 104456 | tf_op jit(solution)/shard_map/ppermute | solution.py:22
  249.8 3.8 %copy-start.2 = (bf16[32]{0:T(256)(128)(2,1)S(1)}, bf16[32]{0:T(256)(128)(2,1)}, u32[]{:S(2)}) copy-start(bf16[32]{0:T(256)(128)(2,1)} %param.11) | copy-start | bytes 196
Sparse Core Ops, SparseCore 0:
  9.6 117.4 all-reduce.1
where the time goes:
time: 262 us; the launch traced here: 261 us
  waiting for transfers between devices  162 us (62%)
  starting transfers between devices  32.9 us (13%)
  local copies, waits for them, and re-layouts  25.1 us (10%)
  matrix products  21.6 us (8%)
  between operations  13.7 us (5%)
  other arithmetic  5.54 us (2%)
    psum x1, waiting for transfers between devices, spread(): return lax.psum(kept, axis)  118 us
    ppermute x6, waiting for transfers between devices, extended(): lax.ppermute(head, axis, [((i + 1) % count, i) for i in range(ends)])  32 us
    conv_general_dilated x9, local copies, waits for them, and re-layouts, dilated_level(): lax.conv_general_dilated(padded[None], weight, (1, 1), 'VALID', rhs_dilat...  22.7 us
    conv_general_dilated x3, matrix products, dilated_level(): lax.conv_general_dilated(padded[None], weight, (1, 1), 'VALID', rhs_dilat...  18.7 us
    ppermute x6, starting transfers between devices, extended(): lax.ppermute(tail, axis, [(i, (i + 1) % count) for i in range(ends)])  18.3 us
    ppermute x6, starting transfers between devices, extended(): lax.ppermute(head, axis, [((i + 1) % count, i) for i in range(ends)])  14.6 us
    ppermute x6, waiting for transfers between devices, extended(): lax.ppermute(tail, axis, [(i, (i + 1) % count) for i in range(ends)])  12.5 us
  transfers between devices with their start and end apart: 13, of which 10 were waited for; matrix products, arithmetic and copies ran while one was open for 0% of the time, Pallas kernels for 0%

commit v1 on v0

v1 whole, which is shorter than its diff:
```python
import jax
import jax.numpy as jnp
from jax import lax
from jax.experimental import pallas as pl
from jax.experimental.pallas import tpu as pltpu
from jax.sharding import PartitionSpec as P

CH = 32
ROWS = 128
COLS = 64
LANES = 128
HALO = 7
TALL = ROWS + 2 * HALO
GROUP = 6
SPAN = GROUP + 2
SIDE = 32
DILATIONS = (1, 2, 4)


def exchange_kernel(emb_ref, row_w_ref, col_w_ref, out_ref, own, land, send_sem, recv_sem):
    n = lax.axis_size("row")
    m = lax.axis_size("col")
    r = lax.axis_index("row")
    c = lax.axis_index("col")
    half = c % 2
    owner = c // 2
    side = owner - 1 + 2 * half
    has_side = jnp.logical_and(side >= 0, side < n)
    is_owner = r == owner
    is_side = r == side
    barrier = pltpu.get_barrier_semaphore()

    def greet(row):
        pl.semaphore_signal(
            barrier, inc=1, device_id=(row, c), device_id_type=pl.DeviceIdType.MESH
        )

    pl.when(r > 0)(lambda: greet(r - 1))
    pl.when(r < n - 1)(lambda: greet(r + 1))
    pl.when(jnp.logical_not(is_owner))(lambda: greet(owner))
    pl.when(jnp.logical_and(has_side, jnp.logical_not(is_side)))(lambda: greet(side))

    for at, w_ref in enumerate((row_w_ref, col_w_ref)):
        own[at] = lax.dot_general(
            w_ref[...], emb_ref[...], (((0,), (1,)), ((), ())), preferred_element_type=jnp.float32
        ).astype(jnp.bfloat16)

    expected = (
        jnp.where(r > 0, 1, 0)
        + jnp.where(r < n - 1, 1, 0)
        + jnp.where(is_owner, n - 1, 0)
        + jnp.where(is_side, n - 1, 0)
    )
    pl.semaphore_wait(barrier, expected)

    def copy(source, slot, row, sem):
        return pltpu.make_async_remote_copy(
            src_ref=own.at[source],
            dst_ref=land.at[slot],
            send_sem=send_sem.at[sem],
            recv_sem=recv_sem.at[slot],
            device_id=(row, c),
            device_id_type=pl.DeviceIdType.MESH,
        )

    def broadcast(slot):
        order = sorted(range(1, n), key=lambda k: -min(k, n - k))
        for k in order:
            copy(1, slot, (r + k) % n, 1 + k).start()

    def finish():
        for k in range(1, n):
            copy(1, 2, (r + k) % n, 1 + k).wait_send()

    pl.when(is_owner)(lambda: broadcast(2))
    pl.when(is_side)(lambda: broadcast(3))
    pl.when(r > 0)(lambda: copy(0, 1, r - 1, 0).start())
    pl.when(r < n - 1)(lambda: copy(0, 0, r + 1, 1).start())

    def fill(slot, value):
        land[slot] = value

    blank = jnp.zeros((CH, LANES), jnp.bfloat16)
    pl.when(is_owner)(lambda: fill(2, own[1]))
    pl.when(is_side)(lambda: fill(3, own[1]))
    pl.when(jnp.logical_not(has_side))(lambda: fill(3, blank))
    pl.when(r == 0)(lambda: fill(0, blank))
    pl.when(r == n - 1)(lambda: fill(1, blank))

    pl.when(r > 0)(lambda: copy(0, 0, r - 1, 0).wait_recv())
    pl.when(r < n - 1)(lambda: copy(0, 1, r + 1, 1).wait_recv())
    pl.when(jnp.logical_not(is_owner))(lambda: copy(1, 2, owner, 2).wait_recv())
    pl.when(jnp.logical_and(has_side, jnp.logical_not(is_side)))(
        lambda: copy(1, 3, side, 2).wait_recv()
    )
    for slot in range(4):
        out_ref[slot] = land[slot]
    out_ref[4] = own[0]
    pl.when(r > 0)(lambda: copy(0, 1, r - 1, 0).wait_send())
    pl.when(r < n - 1)(lambda: copy(0, 0, r + 1, 1).wait_send())
    pl.when(jnp.logical_or(is_owner, is_side))(finish)


def starts(level):
    dilation = DILATIONS[level]
    reach = sum(DILATIONS[: level + 1])
    first, last = reach, TALL - reach
    found = []
    for phase in range(dilation):
        rows = list(range(first + phase, last, dilation))
        at = 0
        while at < len(rows):
            at = min(at, len(rows) - GROUP)
            found.append(rows[at])
            at += GROUP
    return found


def map_kernel(feat_ref, w_ref, bias_ref, head_ref, out_ref, xa, xb, toep, gathered):
    n = lax.axis_size("row")
    m = lax.axis_size("col")
    r = lax.axis_index("row")
    c = lax.axis_index("col")
    half = c % 2
    f32, bf16 = jnp.float32, jnp.bfloat16

    for at in range(9):
        base = w_ref[at].astype(f32)
        for p in range(GROUP):
            moved = base if p == 0 else pltpu.roll(base, CH * p, 1)
            toep[at, p * CH : (p + 1) * CH, :] = moved.astype(bf16)

    lane = lax.broadcasted_iota(jnp.int32, (CH, LANES), 1)
    column = lane + (c * COLS - SIDE)
    inside = jnp.logical_and(column >= 0, column < m * COLS)
    keep = jnp.where(inside, 1.0, 0.0).astype(bf16)

    col_own = feat_ref[2].astype(f32)
    col_side = feat_ref[3].astype(f32)
    low = jnp.where(lane >= SIDE, pltpu.roll(col_own, SIDE, 1), pltpu.roll(col_side, SIDE, 1))
    high = jnp.where(
        lane < LANES - SIDE,
        pltpu.roll(col_own, LANES - SIDE, 1),
        pltpu.roll(col_side, LANES - SIDE, 1),
    )
    cols = jnp.where(half == 0, low, high)

    def put(ref, row, value, dilation):
        ref[1, row] = value
        wide = value.astype(f32)
        ref[0, row] = pltpu.roll(wide, dilation, 1).astype(bf16)
        ref[2, row] = pltpu.roll(wide, LANES - dilation, 1).astype(bf16)

    def clear(ref, level):
        reach = sum(DILATIONS[:level])

        def top():
            for row in range(reach, HALO):
                for tap in range(3):
                    ref[tap, row] = jnp.zeros((CH, LANES), bf16)

        def bottom():
            for row in range(TALL - HALO, TALL - reach):
                for tap in range(3):
                    ref[tap, row] = jnp.zeros((CH, LANES), bf16)

        pl.when(r == 0)(top)
        pl.when(r == n - 1)(bottom)

    keep_wide = keep.astype(f32)
    shifted = [
        pltpu.roll(cols, DILATIONS[0], 1),
        cols,
        pltpu.roll(cols, LANES - DILATIONS[0], 1),
    ]
    kept = [
        pltpu.roll(keep_wide, DILATIONS[0], 1).astype(bf16),
        keep,
        pltpu.roll(keep_wide, LANES - DILATIONS[0], 1).astype(bf16),
    ]
    for slot, lanes, at in (
        (0, range(LANES - HALO, LANES), 0),
        (4, range(LANES), HALO),
        (1, range(HALO), HALO + ROWS),
    ):
        slab = feat_ref[slot].astype(f32)
        for row, where in enumerate(lanes):
            one = jnp.broadcast_to(slab[:, where : where + 1], (CH, LANES))
            for tap in range(3):
                xa[tap, at + row] = (one + shifted[tap]).astype(bf16) * kept[tap]
    clear(xa, 0)

    diagonal = lax.broadcasted_iota(jnp.int32, (CH, CH), 0) == lax.broadcasted_iota(
        jnp.int32, (CH, CH), 1
    )

    def level_bias(level):
        spread = jnp.where(diagonal, bias_ref[level : level + 1, :], 0.0)
        return jnp.broadcast_to(jnp.sum(spread, axis=1, keepdims=True), (CH, LANES))

    tile_from = lax.broadcasted_iota(jnp.int32, (CH, GROUP * CH), 0)
    tile_to = lax.broadcasted_iota(jnp.int32, (CH, GROUP * CH), 1)
    tiler = jnp.where(tile_to % CH == tile_from, 1.0, 0.0).astype(bf16)
    head_rows = jnp.broadcast_to(head_ref[...].astype(f32), (8, CH)).astype(bf16)
    tiled = jnp.dot(head_rows, tiler, preferred_element_type=f32)
    line = lax.broadcasted_iota(jnp.int32, (8, GROUP * CH), 0)
    spot = lax.broadcasted_iota(jnp.int32, (8, GROUP * CH), 1)
    head = jnp.where(spot // CH == line, tiled, 0.0).astype(bf16)

    def window(ref, tap, start, dilation):
        return jnp.concatenate(
            [ref[tap, start + dilation * (q - 1)] for q in range(SPAN)], axis=0
        )

    refs = (xa, xb, xa)
    for level, dilation in enumerate(DILATIONS):
        source = refs[level]
        bias = level_bias(level)
        bias = jnp.concatenate([bias, bias], axis=1)
        bias = jnp.concatenate([bias] * GROUP, axis=0)
        begun = starts(level)
        for left, right in zip(begun[0::2], begun[1::2]):
            total = None
            for tap in range(3):
                seen = jnp.concatenate(
                    [window(source, tap, left, dilation), window(source, tap, right, dilation)],
                    axis=1,
                )
                part = jnp.dot(toep[level * 3 + tap], seen, preferred_element_type=f32)
                total = part if total is None else total + part
            value = jnp.maximum(total + bias, 0.0).astype(bf16)
            if level < 2:
                for part, start in enumerate((left, right)):
                    for p in range(GROUP):
                        piece = value[p * CH : (p + 1) * CH, part * LANES : (part + 1) * LANES]
                        put(refs[level + 1], start + dilation * p, piece * keep, DILATIONS[level + 1])
            else:
                line_out = jnp.dot(head, value, preferred_element_type=f32)
                for part, start in enumerate((left, right)):
                    for p in range(GROUP):
                        row = start + dilation * p - HALO
                        gathered[row : row + 1, :] = line_out[
                            p : p + 1, part * LANES : (part + 1) * LANES
                        ]
        if level < 2:
            clear(refs[level + 1], level + 1)
    out_ref[...] = pltpu.roll(gathered[...], LANES - SIDE, 1)[:, :COLS]


def body(embeddings, row_weight, col_weight, conv_weights, conv_bias, head_weight):
    n = lax.axis_size("row")
    vmem = pl.BlockSpec(memory_space=pltpu.VMEM)
    feats = pl.pallas_call(
        exchange_kernel,
        out_shape=jax.ShapeDtypeStruct((5, CH, LANES), jnp.bfloat16),
        in_specs=[vmem] * 3,
        out_specs=vmem,
        scratch_shapes=[
            pltpu.VMEM((2, CH, LANES), jnp.bfloat16),
            pltpu.VMEM((4, CH, LANES), jnp.bfloat16),
            pltpu.SemaphoreType.DMA((n + 1,)),
            pltpu.SemaphoreType.DMA((4,)),
        ],
        compiler_params=pltpu.CompilerParams(collective_id=0, has_side_effects=True),
        name="exchange",
    )(embeddings, row_weight, col_weight)
    base = conv_weights.transpose(0, 4, 1, 3, 2).reshape(9, CH, 3 * CH)
    base = jnp.pad(base, ((0, 0), (0, 0), (0, SPAN * CH - 3 * CH)))
    return pl.pallas_call(
        map_kernel,
        out_shape=jax.ShapeDtypeStruct((ROWS, COLS), jnp.float32),
        in_specs=[vmem] * 4,
        out_specs=vmem,
        scratch_shapes=[
            pltpu.VMEM((3, TALL, CH, LANES), jnp.bfloat16),
            pltpu.VMEM((3, TALL, CH, LANES), jnp.bfloat16),
            pltpu.VMEM((9, GROUP * CH, SPAN * CH), jnp.bfloat16),
            pltpu.VMEM((ROWS, LANES), jnp.float32),
        ],
        name="contact",
    )(feats, base, conv_bias, head_weight.reshape(1, CH))


def solution(mesh):
    return jax.shard_map(
        body,
        mesh=mesh,
        in_specs=(P("row", None), P(), P(), P(), P(), P()),
        out_specs=P("row", "col"),
        check_vma=False,
    )
```

time: 262 us -> 31 us (0.12)
  the two profiles are of different devices: /device:TPU:223 before, /device:TPU:27 now
where the time goes in v1:
time: 31 us; the launch traced here: 30.7 us
  Pallas kernels  25.9 us (84%)
  local copies, waits for them, and re-layouts  4.79 us (15%)
    pallas_call x1, Pallas kernels, body(): pl.pallas_call(exchange_kernel, out_shape=jax.ShapeDtypeStruct((5, CH, LA...  17.2 us
    pallas_call x1, Pallas kernels, body(): pl.pallas_call(map_kernel, out_shape=jax.ShapeDtypeStruct((ROWS, COLS), j...  8.75 us
    unnamed x6, local copies, waits for them, and re-layouts  2.26 us
    pallas_call x1, local copies, waits for them, and re-layouts, body(): pl.pallas_call(map_kernel, out_shape=jax.ShapeDtypeStruct((ROWS, COLS), j...  1.54 us
    pad x1, local copies, waits for them, and re-layouts, body(): base = jnp.pad(base, ((0, 0), (0, 0), (0, SPAN * CH - 3 * CH)))  0.68 us

profile of v1, /device:TPU:27, one launch (start us, length us, event | category | flops | bytes accessed | tf_op | source)
XLA Modules:
  0.0 30.7 jit_solution(2633503459634767173)
XLA Ops:
  0.0 0.0 copy-start.1
  0.0 1.5 %copy.11.row_w_ref = bf16[512,32]{1,0:T(8,128)(2,1)} copy(bf16[512,32]{0,1:T(8,128)(2,1)} %param.7) | data formatting | bytes 65536 | tf_op args[1]
  1.5 0.0 copy-done.1
  1.5 0.7 %copy.12.col_w_ref = bf16[512,32]{1,0:T(8,128)(2,1)} copy(bf16[512,32]{0,1:T(8,128)(2,1)S(1)} %copy-done.1) | data formatting | bytes 65536 | tf_op args[2]
  2.3 0.0 copy-start
  2.3 17.2 %exchange.1.feat_ref = bf16[5,32,128]{2,1,0:T(8,128)(2,1)} custom-call(bf16[128,512]{1,0:T(8,128)(2,1)} %emb_ref.1, bf16[512,32]{1,0:T(8,128)(2,1)} %copy.11.row_w_ref, bf16[512,32]{1,0:T(8,128)(2,1)} %copy.12.col_w_ref), custom_call_target="tpu_custom_call" | custom-call | tf_op jit(solution)/shard_map/exchange/pallas_call | solution.py:253
  19.4 0.0 copy-done
  19.4 0.2 copy.13
  19.6 0.2 reshape.6
  19.8 0.7 %pad.4.w_ref = bf16[9,32,256]{2,1,0:T(8,128)(2,1)} pad(bf16[9,32,96]{2,1,0:T(8,128)(2,1)S(1)} %reshape.6, bf16[]{:T(256)} %constant.2.clone.1), padding=0_0x0_0x0_160 | pad | bytes 202754 | tf_op jit(solution)/shard_map/jit(_pad)/pad | solution.py:268
  20.5 8.8 %contact.1 = f32[128,64]{1,0:T(8,128)} custom-call(bf16[5,32,128]{2,1,0:T(8,128)(2,1)} %exchange.1.feat_ref, bf16[9,32,256]{2,1,0:T(8,128)(2,1)} %pad.4.w_ref, f32[3,32]{1,0:T(4,128)} %bias_ref.1, bf16[1,32]{1,0:T(2,128)(2,1)} %bitcast.3), custom_call_target="tpu_custom_call" | custom-call | tf_op jit(solution)/shard_map/contact/pallas_call | solution.py:269
  29.2 1.5 %copy.14 = f32[128,64]{0,1:T(8,128)} copy(f32[128,64]{1,0:T(8,128)} %contact.1) | data formatting | bytes 65536 | tf_op jit(solution)/shard_map/contact/pallas_call | solution.py:269
Async XLA Ops:
  0.0 1.5 %copy-start.1 = (bf16[512,32]{0,1:T(8,128)(2,1)S(1)}, bf16[512,32]{0,1:T(8,128)(2,1)}, u32[]{:S(2)}) copy-start(bf16[512,32]{0,1:T(8,128)(2,1)} %param.8) | copy-start | bytes 98308
  2.3 17.2 %copy-start = (bf16[3,32,32,3,3]{2,1,4,3,0:T(8,128)(2,1)S(1)}, bf16[3,32,32,3,3]{2,1,4,3,0:T(8,128)(2,1)}, u32[]{:S(2)}) copy-start(bf16[3,32,32,3,3]{2,1,4,3,0:T(8,128)(2,1)} %param.9) | copy-start | bytes 165892

commit v2 on v1

--- a/solution.py
+++ b/solution.py
@@ -17,7 +17,36 @@
 DILATIONS = (1, 2, 4)
 
 
-def exchange_kernel(emb_ref, row_w_ref, col_w_ref, out_ref, own, land, send_sem, recv_sem):
+def exchange_kernel(
+    emb_hbm,
+    row_w_hbm,
+    col_w_hbm,
+    w_hbm,
+    out_ref,
+    toep,
+    emb_ref,
+    proj_ref,
+    w_ref,
+    own,
+    land,
+    load_sem,
+    send_sem,
+    recv_sem,
+):
+    loads = [
+        pltpu.make_async_copy(source, target, load_sem.at[at])
+        for at, (source, target) in enumerate(
+            (
+                (emb_hbm, emb_ref),
+                (row_w_hbm, proj_ref.at[0]),
+                (col_w_hbm, proj_ref.at[1]),
+                (w_hbm, w_ref),
+            )
+        )
+    ]
+    for load in loads:
+        load.start()
+
     n = lax.axis_size("row")
     m = lax.axis_size("col")
     r = lax.axis_index("row")
@@ -40,10 +69,16 @@
     pl.when(jnp.logical_not(is_owner))(lambda: greet(owner))
     pl.when(jnp.logical_and(has_side, jnp.logical_not(is_side)))(lambda: greet(side))
 
-    for at, w_ref in enumerate((row_w_ref, col_w_ref)):
-        own[at] = lax.dot_general(
-            w_ref[...], emb_ref[...], (((0,), (1,)), ((), ())), preferred_element_type=jnp.float32
-        ).astype(jnp.bfloat16)
+    for load in loads[:3]:
+        load.wait()
+    projected = lax.dot_general(
+        jnp.concatenate([proj_ref[0], proj_ref[1]], axis=0),
+        emb_ref[...],
+        (((1,), (1,)), ((), ())),
+        preferred_element_type=jnp.float32,
+    ).astype(jnp.bfloat16)
+    own[0] = projected[:CH]
+    own[1] = projected[CH:]
 
     expected = (
         jnp.where(r > 0, 1, 0)
@@ -86,6 +121,16 @@
     pl.when(jnp.logical_not(has_side))(lambda: fill(3, blank))
     pl.when(r == 0)(lambda: fill(0, blank))
     pl.when(r == n - 1)(lambda: fill(1, blank))
+
+    toep[...] = jnp.zeros_like(toep)
+    loads[3].wait()
+    for level in range(3):
+        for b in range(3):
+            for a in range(3):
+                tap = w_ref[level, a, b]
+                for p in range(GROUP):
+                    at = CH * (p + a)
+                    toep[level * 3 + b, p * CH : (p + 1) * CH, at : at + CH] = tap
 
     pl.when(r > 0)(lambda: copy(0, 0, r - 1, 0).wait_recv())
     pl.when(r < n - 1)(lambda: copy(0, 1, r + 1, 1).wait_recv())
@@ -116,19 +161,13 @@
     return found
 
 
-def map_kernel(feat_ref, w_ref, bias_ref, head_ref, out_ref, xa, xb, toep, gathered):
+def map_kernel(feat_ref, toep, bias_ref, head_ref, out_ref, xa, xb, gathered):
     n = lax.axis_size("row")
     m = lax.axis_size("col")
     r = lax.axis_index("row")
     c = lax.axis_index("col")
     half = c % 2
     f32, bf16 = jnp.float32, jnp.bfloat16
-
-    for at in range(9):
-        base = w_ref[at].astype(f32)
-        for p in range(GROUP):
-            moved = base if p == 0 else pltpu.roll(base, CH * p, 1)
-            toep[at, p * CH : (p + 1) * CH, :] = moved.astype(bf16)
 
     lane = lax.broadcasted_iota(jnp.int32, (CH, LANES), 1)
     column = lane + (c * COLS - SIDE)
@@ -244,41 +283,49 @@
                         ]
         if level < 2:
             clear(refs[level + 1], level + 1)
-    out_ref[...] = pltpu.roll(gathered[...], LANES - SIDE, 1)[:, :COLS]
+    out_ref[...] = gathered[...].T[SIDE : SIDE + COLS]
 
 
 def body(embeddings, row_weight, col_weight, conv_weights, conv_bias, head_weight):
     n = lax.axis_size("row")
     vmem = pl.BlockSpec(memory_space=pltpu.VMEM)
-    feats = pl.pallas_call(
+    feats, banded = pl.pallas_call(
         exchange_kernel,
-        out_shape=jax.ShapeDtypeStruct((5, CH, LANES), jnp.bfloat16),
-        in_specs=[vmem] * 3,
-        out_specs=vmem,
+        out_shape=(
+            jax.ShapeDtypeStruct((5, CH, LANES), jnp.bfloat16),
+            jax.ShapeDtypeStruct((9, GROUP * CH, SPAN * CH), jnp.bfloat16),
+        ),
+        in_specs=[pl.BlockSpec(memory_space=pltpu.HBM)] * 4,
+        out_specs=(vmem, vmem),
         scratch_shapes=[
+            pltpu.VMEM(embeddings.shape, jnp.bfloat16),
+            pltpu.VMEM((2, CH, embeddings.shape[1]), jnp.bfloat16),
+            pltpu.VMEM((3, 3, 3, CH, CH), jnp.bfloat16),
             pltpu.VMEM((2, CH, LANES), jnp.bfloat16),
             pltpu.VMEM((4, CH, LANES), jnp.bfloat16),
+            pltpu.SemaphoreType.DMA((4,)),
             pltpu.SemaphoreType.DMA((n + 1,)),
             pltpu.SemaphoreType.DMA((4,)),
         ],
-        compiler_params=pltpu.CompilerParams(collective_id=0, has_side_effects=True),
+        compiler_params=pltpu.CompilerParams(
+            collective_id=0, has_side_effects=True, vmem_limit_bytes=16 * 2**20
+        ),
         name="exchange",
-    )(embeddings, row_weight, col_weight)
-    base = conv_weights.transpose(0, 4, 1, 3, 2).reshape(9, CH, 3 * CH)
-    base = jnp.pad(base, ((0, 0), (0, 0), (0, SPAN * CH - 3 * CH)))
-    return pl.pallas_call(
+    )(embeddings, row_weight.T, col_weight.T, conv_weights.transpose(0, 3, 4, 1, 2))
+    contact = pl.pallas_call(
         map_kernel,
-        out_shape=jax.ShapeDtypeStruct((ROWS, COLS), jnp.float32),
+        out_shape=jax.ShapeDtypeStruct((COLS, ROWS), jnp.float32),
         in_specs=[vmem] * 4,
         out_specs=vmem,
         scratch_shapes=[
             pltpu.VMEM((3, TALL, CH, LANES), jnp.bfloat16),
             pltpu.VMEM((3, TALL, CH, LANES), jnp.bfloat16),
-            pltpu.VMEM((9, GROUP * CH, SPAN * CH), jnp.bfloat16),
             pltpu.VMEM((ROWS, LANES), jnp.float32),
         ],
+        compiler_params=pltpu.CompilerParams(vmem_limit_bytes=24 * 2**20),
         name="contact",
-    )(feats, base, conv_bias, head_weight.reshape(1, CH))
+    )(feats, banded, conv_bias, head_weight.reshape(1, CH))
+    return contact.T
 
 
 def solution(mesh):

time: 31 us -> 28.1 us (0.906)
  Pallas kernels: 25.9 us -> 23.8 us
  local copies, waits for them, and re-layouts: 4.79 us -> 4.02 us
    pallas_call x2, Pallas kernels: 25.9 us -> 23.8 us  [the longest x1 16 us: body(): pl.pallas_call(exchange_kernel, out_shape=(jax.ShapeDtypeStruct((5, CH, L...]
    unnamed x6 -> x12, local copies, waits for them, and re-layouts: 2.26 us -> 4.02 us
    pallas_call x1 -> x0, local copies, waits for them, and re-layouts: 1.54 us -> none  [body(): pl.pallas_call(map_kernel, out_shape=jax.ShapeDtypeStruct((ROWS, COLS), j...]
    pad x1 -> x0, local copies, waits for them, and re-layouts: 0.68 us -> none  [body(): base = jnp.pad(base, ((0, 0), (0, 0), (0, SPAN * CH - 3 * CH)))]
where the time goes in v2:
time: 28.1 us; the launch traced here: 27.8 us
  Pallas kernels  23.8 us (85%)
  local copies, waits for them, and re-layouts  4.02 us (14%)
    pallas_call x1, Pallas kernels, body(): pl.pallas_call(exchange_kernel, out_shape=(jax.ShapeDtypeStruct((5, CH, L...  16 us
    pallas_call x1, Pallas kernels, body(): pl.pallas_call(map_kernel, out_shape=jax.ShapeDtypeStruct((COLS, ROWS), j...  7.75 us
    unnamed x12, local copies, waits for them, and re-layouts  4.02 us

profile of v2, /device:TPU:27, one launch (start us, length us, event | category | flops | bytes accessed | tf_op | source)
XLA Modules:
  0.0 27.8 jit_solution(15596115283401892243)
XLA Ops:
  0.0 0.0 copy-start
  0.0 0.9 %copy-done = bf16[3,32,32,3,3]{2,1,4,3,0:T(8,128)(2,1)S(1)} copy-done((bf16[3,32,32,3,3]{2,1,4,3,0:T(8,128)(2,1)S(1)}, bf16[3,32,32,3,3]{2,1,4,3,0:T(8,128)(2,1)}, u32[]{:S(2)}) %copy-start) | copy-done | bytes 55320
  0.9 0.0 copy-start.1
  0.9 0.9 %copy-done.1 = bf16[128,512]{1,0:T(8,128)(2,1)S(1)} copy-done((bf16[128,512]{1,0:T(8,128)(2,1)S(1)}, bf16[128,512]{1,0:T(8,128)(2,1)}, u32[]{:S(2)}) %copy-start.1) | copy-done | bytes 131096
  1.8 0.0 copy-start.2
  1.8 0.8 %copy-done.2 = bf16[512,32]{0,1:T(8,128)(2,1)S(1)} copy-done((bf16[512,32]{0,1:T(8,128)(2,1)S(1)}, bf16[512,32]{0,1:T(8,128)(2,1)}, u32[]{:S(2)}) %copy-start.2) | copy-done | bytes 32792
  2.6 0.0 copy-start.3
  2.6 0.8 %copy-done.3 = bf16[512,32]{0,1:T(8,128)(2,1)S(1)} copy-done((bf16[512,32]{0,1:T(8,128)(2,1)S(1)}, bf16[512,32]{0,1:T(8,128)(2,1)}, u32[]{:S(2)}) %copy-start.3) | copy-done | bytes 32792
  3.4 16.0 %exchange.1 = (bf16[5,32,128]{2,1,0:T(8,128)(2,1)S(1)}, bf16[9,192,256]{2,1,0:T(8,128)(2,1)S(1)}) custom-call(bf16[128,512]{1,0:T(8,128)(2,1)S(1)} %copy-done.1, bf16[32,512]{1,0:T(8,128)(2,1)S(1)} %bitcast.6, bf16[32,512]{1,0:T(8,128)(2,1)S(1)} %bitcast.7, bf16[3,3,3,32,32]{4,3,2,1,0:T(8,128)(2,1)S(1)} %bitcast.5), custom_call_target="tpu_custom_call" | custom-call | tf_op jit(solution)/shard_map/exchange/pallas_call | solution.py:292
  19.4 0.0 copy-start.4
  19.4 0.0 copy-start.5
  19.4 0.7 %copy-done.4 = f32[3,32]{1,0:T(4,128)S(1)} copy-done((f32[3,32]{1,0:T(4,128)S(1)}, f32[3,32]{1,0:T(4,128)}, u32[]{:S(2)}) %copy-start.4) | copy-done | bytes 408
  20.1 0.0 copy-done.5
  20.1 7.7 %contact.1 = f32[64,128]{1,0:T(8,128)} custom-call(bf16[5,32,128]{2,1,0:T(8,128)(2,1)S(1)} %get-tuple-element.7.feat_ref, bf16[9,192,256]{2,1,0:T(8,128)(2,1)S(1)} %get-tuple-element.8.toep, f32[3,32]{1,0:T(4,128)S(1)} %copy-done.4, bf16[1,32]{1,0:T(2,128)(2,1)S(1)} %bitcast.8), custom_call_target="tpu_custom_call" | custom-call | tf_op jit(solution)/shard_map/contact/pallas_call | solution.py:315
Async XLA Ops:
  0.0 0.9 %copy-start = (bf16[3,32,32,3,3]{2,1,4,3,0:T(8,128)(2,1)S(1)}, bf16[3,32,32,3,3]{2,1,4,3,0:T(8,128)(2,1)}, u32[]{:S(2)}) copy-start(bf16[3,32,32,3,3]{2,1,4,3,0:T(8,128)(2,1)} %param.9) | copy-start | bytes 165892
  0.9 0.9 %copy-start.1 = (bf16[128,512]{1,0:T(8,128)(2,1)S(1)}, bf16[128,512]{1,0:T(8,128)(2,1)}, u32[]{:S(2)}) copy-start(bf16[128,512]{1,0:T(8,128)(2,1)} %emb_hbm.1) | copy-start | bytes 393220
  1.8 0.8 %copy-start.2 = (bf16[512,32]{0,1:T(8,128)(2,1)S(1)}, bf16[512,32]{0,1:T(8,128)(2,1)}, u32[]{:S(2)}) copy-start(bf16[512,32]{0,1:T(8,128)(2,1)} %param.7) | copy-start | bytes 98308
  2.6 0.8 %copy-start.3 = (bf16[512,32]{0,1:T(8,128)(2,1)S(1)}, bf16[512,32]{0,1:T(8,128)(2,1)}, u32[]{:S(2)}) copy-start(bf16[512,32]{0,1:T(8,128)(2,1)} %param.8) | copy-start | bytes 98308
  19.4 0.7 %copy-start.4 = (f32[3,32]{1,0:T(4,128)S(1)}, f32[3,32]{1,0:T(4,128)}, u32[]{:S(2)}) copy-start(f32[3,32]{1,0:T(4,128)} %bias_ref.1) | copy-start | bytes 1156
  19.4 0.7 %copy-start.5 = (bf16[32]{0:T(256)(128)(2,1)S(1)}, bf16[32]{0:T(256)(128)(2,1)}, u32[]{:S(2)}) copy-start(bf16[32]{0:T(256)(128)(2,1)} %param.11) | copy-start | bytes 196

commit v3 on v2

v3 whole, which is shorter than its diff:
```python
import jax
import jax.numpy as jnp
from jax import lax
from jax.experimental import pallas as pl
from jax.experimental.pallas import tpu as pltpu
from jax.sharding import PartitionSpec as P

CH = 32
ROWS = 128
COLS = 64
LANES = 128
HALO = 7
TALL = ROWS + 2 * HALO
GROUP = 6
SPAN = GROUP + 2
SIDE = 32
DILATIONS = (1, 2, 4)


def starts(level):
    dilation = DILATIONS[level]
    reach = sum(DILATIONS[: level + 1])
    first, last = reach, TALL - reach
    found = []
    for phase in range(dilation):
        rows = list(range(first + phase, last, dilation))
        at = 0
        while at < len(rows):
            at = min(at, len(rows) - GROUP)
            found.append(rows[at])
            at += GROUP
    return found


def contact_kernel(
    emb_hbm,
    row_w_hbm,
    col_w_hbm,
    w_hbm,
    bias_hbm,
    head_hbm,
    out_ref,
    emb_ref,
    proj_ref,
    w_ref,
    bias_ref,
    head_ref,
    own,
    land,
    toep,
    xa,
    xb,
    last,
    gathered,
    load_sem,
    send_sem,
    recv_sem,
):
    loads = [
        pltpu.make_async_copy(source, target, load_sem.at[at])
        for at, (source, target) in enumerate(
            (
                (emb_hbm, emb_ref),
                (row_w_hbm, proj_ref.at[0]),
                (col_w_hbm, proj_ref.at[1]),
                (w_hbm, w_ref),
                (bias_hbm, bias_ref),
                (head_hbm, head_ref),
            )
        )
    ]
    for load in loads:
        load.start()

    n = lax.axis_size("row")
    m = lax.axis_size("col")
    r = lax.axis_index("row")
    c = lax.axis_index("col")
    half = c % 2
    owner = c // 2
    side = owner - 1 + 2 * half
    has_side = jnp.logical_and(side >= 0, side < n)
    is_owner = r == owner
    is_side = r == side
    barrier = pltpu.get_barrier_semaphore()

    def greet(row):
        pl.semaphore_signal(
            barrier, inc=1, device_id=(row, c), device_id_type=pl.DeviceIdType.MESH
        )

    pl.when(r > 0)(lambda: greet(r - 1))
    pl.when(r < n - 1)(lambda: greet(r + 1))
    pl.when(jnp.logical_not(is_owner))(lambda: greet(owner))
    pl.when(jnp.logical_and(has_side, jnp.logical_not(is_side)))(lambda: greet(side))

    for load in loads[:3]:
        load.wait()
    projected = lax.dot_general(
        jnp.concatenate([proj_ref[0], proj_ref[1]], axis=0),
        emb_ref[...],
        (((1,), (1,)), ((), ())),
        preferred_element_type=jnp.float32,
    ).astype(jnp.bfloat16)
    own[0] = projected[:CH]
    own[1] = projected[CH:]

    expected = (
        jnp.where(r > 0, 1, 0)
        + jnp.where(r < n - 1, 1, 0)
        + jnp.where(is_owner, n - 1, 0)
        + jnp.where(is_side, n - 1, 0)
    )
    pl.semaphore_wait(barrier, expected)

    def copy(source, slot, row, sem):
        return pltpu.make_async_remote_copy(
            src_ref=own.at[source],
            dst_ref=land.at[slot],
            send_sem=send_sem.at[sem],
            recv_sem=recv_sem.at[slot],
            device_id=(row, c),
            device_id_type=pl.DeviceIdType.MESH,
        )

    def broadcast(slot):
        order = sorted(range(1, n), key=lambda k: -min(k, n - k))
        for k in order:
            copy(1, slot, (r + k) % n, 1 + k).start()

    def finish():
        for k in range(1, n):
            copy(1, 2, (r + k) % n, 1 + k).wait_send()

    pl.when(is_owner)(lambda: broadcast(2))
    pl.when(is_side)(lambda: broadcast(3))
    pl.when(r > 0)(lambda: copy(0, 1, r - 1, 0).start())
    pl.when(r < n - 1)(lambda: copy(0, 0, r + 1, 1).start())

    def fill(slot, value):
        land[slot] = value

    blank = jnp.zeros((CH, LANES), jnp.bfloat16)
    pl.when(is_owner)(lambda: fill(2, own[1]))
    pl.when(is_side)(lambda: fill(3, own[1]))
    pl.when(jnp.logical_not(has_side))(lambda: fill(3, blank))
    pl.when(r == 0)(lambda: fill(0, blank))
    pl.when(r == n - 1)(lambda: fill(1, blank))

    toep[...] = jnp.zeros_like(toep)
    for load in loads[3:]:
        load.wait()
    for level in range(3):
        for b in range(3):
            for a in range(3):
                tap = w_ref[level, a, b]
                for p in range(GROUP):
                    at = CH * (p + a)
                    toep[level * 3 + b, p * CH : (p + 1) * CH, at : at + CH] = tap

    f32, bf16 = jnp.float32, jnp.bfloat16
    lane = lax.broadcasted_iota(jnp.int32, (CH, LANES), 1)
    column = lane + (c * COLS - SIDE)
    inside = jnp.logical_and(column >= 0, column < m * COLS)
    keep = jnp.where(inside, 1.0, 0.0)
    above = jnp.where(r > 0, 1.0, 0.0)
    below = jnp.where(r < n - 1, 1.0, 0.0)

    def taps(value, dilation):
        return [
            pltpu.roll(value, dilation, 1),
            value,
            pltpu.roll(value, LANES - dilation, 1),
        ]

    def masks(dilation):
        return [
            [part.astype(bf16) for part in taps(keep * edge, dilation)]
            for edge in (above, 1.0, below)
        ]

    def zone(row):
        return 0 if row < HALO else (1 if row < HALO + ROWS else 2)

    def row_band(slot_value, where):
        return jnp.broadcast_to(slot_value[:, where : where + 1], (CH, LANES)).astype(bf16)

    mine = own[0].astype(f32)
    for row in range(ROWS):
        xb[1, HALO + row] = row_band(mine, row)

    diagonal = lax.broadcasted_iota(jnp.int32, (CH, CH), 0) == lax.broadcasted_iota(
        jnp.int32, (CH, CH), 1
    )

    def level_bias(level):
        spread = jnp.where(diagonal, bias_ref[level : level + 1, :], 0.0)
        one = jnp.broadcast_to(jnp.sum(spread, axis=1, keepdims=True), (CH, LANES))
        one = jnp.concatenate([one, one], axis=1)
        return jnp.concatenate([one] * GROUP, axis=0)

    biases = [level_bias(level) for level in range(3)]
    tile_from = lax.broadcasted_iota(jnp.int32, (CH, SPAN * CH), 0)
    tile_to = lax.broadcasted_iota(jnp.int32, (CH, SPAN * CH), 1)
    tiler = jnp.where(tile_to % CH == tile_from, 1.0, 0.0).astype(bf16)
    head_rows = jnp.broadcast_to(head_ref[...].astype(f32), (8, CH)).astype(bf16)
    tiled = jnp.dot(head_rows, tiler, preferred_element_type=f32)
    line = lax.broadcasted_iota(jnp.int32, (8, SPAN * CH), 0)
    spot = lax.broadcasted_iota(jnp.int32, (8, SPAN * CH), 1)
    head = jnp.where(spot // CH == line, tiled, 0.0).astype(bf16)

    pl.when(r > 0)(lambda: copy(0, 0, r - 1, 0).wait_recv())
    pl.when(r < n - 1)(lambda: copy(0, 1, r + 1, 1).wait_recv())
    pl.when(jnp.logical_not(is_owner))(lambda: copy(1, 2, owner, 2).wait_recv())
    pl.when(jnp.logical_and(has_side, jnp.logical_not(is_side)))(
        lambda: copy(1, 3, side, 2).wait_recv()
    )

    col_own = land[2].astype(f32)
    col_side = land[3].astype(f32)
    low = jnp.where(lane >= SIDE, pltpu.roll(col_own, SIDE, 1), pltpu.roll(col_side, SIDE, 1))
    high = jnp.where(
        lane < LANES - SIDE,
        pltpu.roll(col_own, LANES - SIDE, 1),
        pltpu.roll(col_side, LANES - SIDE, 1),
    )
    cols = [part.astype(bf16) for part in taps(jnp.where(half == 0, low, high), DILATIONS[0])]
    kept = masks(DILATIONS[0])
    before = land[0].astype(f32)
    after = land[1].astype(f32)
    for row in range(TALL):
        if zone(row) == 0:
            one = row_band(before, LANES - HALO + row)
        elif zone(row) == 2:
            one = row_band(after, row - HALO - ROWS)
        else:
            one = xb[1, row]
        for tap in range(3):
            xa[tap, row] = (one + cols[tap]) * kept[zone(row)][tap]

    def window(ref, tap, start, dilation):
        return jnp.concatenate(
            [ref[tap, start + dilation * (q - 1)] for q in range(SPAN)], axis=0
        )

    refs = (xa, xb, xa)
    for level, dilation in enumerate(DILATIONS):
        source = refs[level]
        if level < 2:
            kept = masks(DILATIONS[level + 1])
        begun = starts(level)
        for left, right in zip(begun[0::2], begun[1::2]):
            total = None
            for tap in range(3):
                seen = jnp.concatenate(
                    [window(source, tap, left, dilation), window(source, tap, right, dilation)],
                    axis=1,
                )
                part = jnp.dot(toep[level * 3 + tap], seen, preferred_element_type=f32)
                total = part if total is None else total + part
            value = jnp.maximum(total + biases[level], 0.0)
            for half_at, start in enumerate((left, right)):
                for p in range(GROUP):
                    row = start + dilation * p
                    piece = value[
                        p * CH : (p + 1) * CH, half_at * LANES : (half_at + 1) * LANES
                    ]
                    if level == 2:
                        last[row - HALO] = piece.astype(bf16)
                        continue
                    for tap, moved in enumerate(taps(piece, DILATIONS[level + 1])):
                        refs[level + 1][tap, row] = moved.astype(bf16) * kept[zone(row)][tap]
    for at in range(0, ROWS, 16):
        seen = jnp.concatenate(
            [
                jnp.concatenate([last[at + first + q] for q in range(SPAN)], axis=0)
                for first in (0, SPAN)
            ],
            axis=1,
        )
        lines = jnp.dot(head, seen, preferred_element_type=f32)
        gathered[at : at + SPAN] = lines[:, :LANES]
        gathered[at + SPAN : at + 2 * SPAN] = lines[:, LANES:]
    out_ref[...] = gathered[...].T[SIDE : SIDE + COLS]
    pl.when(r > 0)(lambda: copy(0, 1, r - 1, 0).wait_send())
    pl.when(r < n - 1)(lambda: copy(0, 0, r + 1, 1).wait_send())
    pl.when(jnp.logical_or(is_owner, is_side))(finish)


def body(embeddings, row_weight, col_weight, conv_weights, conv_bias, head_weight):
    n = lax.axis_size("row")
    vmem = pl.BlockSpec(memory_space=pltpu.VMEM)
    contact = pl.pallas_call(
        contact_kernel,
        out_shape=jax.ShapeDtypeStruct((COLS, ROWS), jnp.float32),
        in_specs=[pl.BlockSpec(memory_space=pltpu.HBM)] * 6,
        out_specs=vmem,
        scratch_shapes=[
            pltpu.VMEM(embeddings.shape, jnp.bfloat16),
            pltpu.VMEM((2, CH, embeddings.shape[1]), jnp.bfloat16),
            pltpu.VMEM((3, 3, 3, CH, CH), jnp.bfloat16),
            pltpu.VMEM((3, CH), jnp.float32),
            pltpu.VMEM((1, CH), jnp.bfloat16),
            pltpu.VMEM((2, CH, LANES), jnp.bfloat16),
            pltpu.VMEM((4, CH, LANES), jnp.bfloat16),
            pltpu.VMEM((9, GROUP * CH, SPAN * CH), jnp.bfloat16),
            pltpu.VMEM((3, TALL, CH, LANES), jnp.bfloat16),
            pltpu.VMEM((3, TALL, CH, LANES), jnp.bfloat16),
            pltpu.VMEM((ROWS, CH, LANES), jnp.bfloat16),
            pltpu.VMEM((ROWS, LANES), jnp.float32),
            pltpu.SemaphoreType.DMA((6,)),
            pltpu.SemaphoreType.DMA((n + 1,)),
            pltpu.SemaphoreType.DMA((4,)),
        ],
        compiler_params=pltpu.CompilerParams(collective_id=0, has_side_effects=True),
        name="contact",
    )(
        embeddings,
        row_weight.T,
        col_weight.T,
        conv_weights.transpose(0, 3, 4, 1, 2),
        conv_bias,
        head_weight.reshape(1, CH),
    )
    return contact.T


def solution(mesh):
    return jax.shard_map(
        body,
        mesh=mesh,
        in_specs=(P("row", None), P(), P(), P(), P(), P()),
        out_specs=P("row", "col"),
        check_vma=False,
    )
```

time: 28.1 us -> 21.9 us (0.78)
  Pallas kernels: 23.8 us -> 20.3 us
  local copies, waits for them, and re-layouts: 4.02 us -> 1.38 us
    pallas_call x2 -> x1, Pallas kernels: 23.8 us -> 20.3 us  [body(): pl.pallas_call(contact_kernel, out_shape=jax.ShapeDtypeStruct((COLS, ROWS...]
    unnamed x12 -> x1, local copies, waits for them, and re-layouts: 4.02 us -> 1.38 us
where the time goes in v3:
time: 21.9 us; the launch traced here: 21.7 us
  Pallas kernels  20.3 us (93%)
  local copies, waits for them, and re-layouts  1.38 us (6%)
    pallas_call x1, Pallas kernels, body(): pl.pallas_call(contact_kernel, out_shape=jax.ShapeDtypeStruct((COLS, ROWS...  20.3 us
    unnamed x1, local copies, waits for them, and re-layouts  1.38 us

profile of v3, /device:TPU:27, one launch (start us, length us, event | category | flops | bytes accessed | tf_op | source)
XLA Modules:
  0.0 21.7 jit_solution(6209308023448924995)
XLA Ops:
  0.0 20.3 %contact.1 = f32[64,128]{1,0:T(8,128)} custom-call(bf16[128,512]{1,0:T(8,128)(2,1)} %emb_hbm.1, bf16[32,512]{1,0:T(8,128)(2,1)} %bitcast.7, bf16[32,512]{1,0:T(8,128)(2,1)} %bitcast.8, bf16[3,3,3,32,32]{4,3,2,1,0:T(8,128)(2,1)} %bitcast.5, f32[3,32]{1,0:T(4,128)} %bias_hbm.1, bf16[1,32]{1,0:T(2,128)(2,1)} %bitcast.9), custom_call_target="tpu_custom_call" | custom-call | tf_op jit(solution)/shard_map/contact/pallas_call | solution.py:293
  20.3 1.4 %copy.8 = f32[128,64]{0,1:T(8,128)} copy(f32[128,64]{0,1:T(8,128)} %bitcast.6) | data formatting | bytes 65536

commit v4 on v3

--- a/solution.py
+++ b/solution.py
@@ -29,7 +29,7 @@
             at = min(at, len(rows) - GROUP)
             found.append(rows[at])
             at += GROUP
-    return found
+    return sorted(found)
 
 
 def contact_kernel(
@@ -48,6 +48,7 @@
     own,
     land,
     toep,
+    band,
     xa,
     xb,
     last,
@@ -173,11 +174,11 @@
             pltpu.roll(value, LANES - dilation, 1),
         ]
 
-    def masks(dilation):
-        return [
-            [part.astype(bf16) for part in taps(keep * edge, dilation)]
-            for edge in (above, 1.0, below)
-        ]
+    kept = [
+        [part.astype(bf16) for part in taps(keep * edge, DILATIONS[0])]
+        for edge in (above, 1.0, below)
+    ]
+    shut = -3.0e38
 
     def zone(row):
         return 0 if row < HALO else (1 if row < HALO + ROWS else 2)
@@ -187,7 +188,9 @@
 
     mine = own[0].astype(f32)
     for row in range(ROWS):
-        xb[1, HALO + row] = row_band(mine, row)
+        one = row_band(mine, row)
+        for tap in range(3):
+            band[tap, row] = one * kept[1][tap]
 
     diagonal = lax.broadcasted_iota(jnp.int32, (CH, CH), 0) == lax.broadcasted_iota(
         jnp.int32, (CH, CH), 1
@@ -196,8 +199,10 @@
     def level_bias(level):
         spread = jnp.where(diagonal, bias_ref[level : level + 1, :], 0.0)
         one = jnp.broadcast_to(jnp.sum(spread, axis=1, keepdims=True), (CH, LANES))
-        one = jnp.concatenate([one, one], axis=1)
-        return jnp.concatenate([one] * GROUP, axis=0)
+        if level == 2:
+            return [one] * 3
+        one = jnp.where(inside, one, shut)
+        return [jnp.where(r > 0, one, shut), one, jnp.where(r < n - 1, one, shut)]
 
     biases = [level_bias(level) for level in range(3)]
     tile_from = lax.broadcasted_iota(jnp.int32, (CH, SPAN * CH), 0)
@@ -225,7 +230,7 @@
         pltpu.roll(col_side, LANES - SIDE, 1),
     )
     cols = [part.astype(bf16) for part in taps(jnp.where(half == 0, low, high), DILATIONS[0])]
-    kept = masks(DILATIONS[0])
+    cols_kept = [cols[tap] * kept[1][tap] for tap in range(3)]
     before = land[0].astype(f32)
     after = land[1].astype(f32)
     for row in range(TALL):
@@ -234,7 +239,9 @@
         elif zone(row) == 2:
             one = row_band(after, row - HALO - ROWS)
         else:
-            one = xb[1, row]
+            for tap in range(3):
+                xa[tap, row] = band[tap, row - HALO] + cols_kept[tap]
+            continue
         for tap in range(3):
             xa[tap, row] = (one + cols[tap]) * kept[zone(row)][tap]
 
@@ -243,11 +250,21 @@
             [ref[tap, start + dilation * (q - 1)] for q in range(SPAN)], axis=0
         )
 
+    def apply_head(at):
+        seen = jnp.concatenate(
+            [
+                jnp.concatenate([last[at + first + q] for q in range(SPAN)], axis=0)
+                for first in (0, SPAN)
+            ],
+            axis=1,
+        )
+        lines = jnp.dot(head, seen, preferred_element_type=f32)
+        gathered[at : at + SPAN] = lines[:, :LANES]
+        gathered[at + SPAN : at + 2 * SPAN] = lines[:, LANES:]
+
     refs = (xa, xb, xa)
     for level, dilation in enumerate(DILATIONS):
         source = refs[level]
-        if level < 2:
-            kept = masks(DILATIONS[level + 1])
         begun = starts(level)
         for left, right in zip(begun[0::2], begun[1::2]):
             total = None
@@ -258,29 +275,20 @@
                 )
                 part = jnp.dot(toep[level * 3 + tap], seen, preferred_element_type=f32)
                 total = part if total is None else total + part
-            value = jnp.maximum(total + biases[level], 0.0)
             for half_at, start in enumerate((left, right)):
                 for p in range(GROUP):
                     row = start + dilation * p
-                    piece = value[
+                    piece = total[
                         p * CH : (p + 1) * CH, half_at * LANES : (half_at + 1) * LANES
                     ]
+                    piece = jnp.maximum(piece + biases[level][zone(row)], 0.0)
                     if level == 2:
                         last[row - HALO] = piece.astype(bf16)
                         continue
                     for tap, moved in enumerate(taps(piece, DILATIONS[level + 1])):
-                        refs[level + 1][tap, row] = moved.astype(bf16) * kept[zone(row)][tap]
-    for at in range(0, ROWS, 16):
-        seen = jnp.concatenate(
-            [
-                jnp.concatenate([last[at + first + q] for q in range(SPAN)], axis=0)
-                for first in (0, SPAN)
-            ],
-            axis=1,
-        )
-        lines = jnp.dot(head, seen, preferred_element_type=f32)
-        gathered[at : at + SPAN] = lines[:, :LANES]
-        gathered[at + SPAN : at + 2 * SPAN] = lines[:, LANES:]
+                        refs[level + 1][tap, row] = moved.astype(bf16)
+    for at in range(0, ROWS, 2 * SPAN):
+        apply_head(at)
     out_ref[...] = gathered[...].T[SIDE : SIDE + COLS]
     pl.when(r > 0)(lambda: copy(0, 1, r - 1, 0).wait_send())
     pl.when(r < n - 1)(lambda: copy(0, 0, r + 1, 1).wait_send())
@@ -304,6 +312,7 @@
             pltpu.VMEM((2, CH, LANES), jnp.bfloat16),
             pltpu.VMEM((4, CH, LANES), jnp.bfloat16),
             pltpu.VMEM((9, GROUP * CH, SPAN * CH), jnp.bfloat16),
+            pltpu.VMEM((3, ROWS, CH, LANES), jnp.bfloat16),
             pltpu.VMEM((3, TALL, CH, LANES), jnp.bfloat16),
             pltpu.VMEM((3, TALL, CH, LANES), jnp.bfloat16),
             pltpu.VMEM((ROWS, CH, LANES), jnp.bfloat16),

time: 21.9 us -> 21.1 us (0.963)
  Pallas kernels: 20.3 us -> 19.6 us
    pallas_call x1, Pallas kernels: 20.3 us -> 19.6 us  [body(): pl.pallas_call(contact_kernel, out_shape=jax.ShapeDtypeStruct((COLS, ROWS...]
where the time goes in v4:
time: 21.1 us; the launch traced here: 20.9 us
  Pallas kernels  19.6 us (93%)
  local copies, waits for them, and re-layouts  1.38 us (7%)
    pallas_call x1, Pallas kernels, body(): pl.pallas_call(contact_kernel, out_shape=jax.ShapeDtypeStruct((COLS, ROWS...  19.6 us
    unnamed x1, local copies, waits for them, and re-layouts  1.38 us

profile of v4, /device:TPU:27, one launch (start us, length us, event | category | flops | bytes accessed | tf_op | source)
XLA Modules:
  0.0 20.9 jit_solution(7272664088960875930)
XLA Ops:
  0.0 19.6 %contact.1 = f32[64,128]{1,0:T(8,128)} custom-call(bf16[128,512]{1,0:T(8,128)(2,1)} %emb_hbm.1, bf16[32,512]{1,0:T(8,128)(2,1)} %bitcast.7, bf16[32,512]{1,0:T(8,128)(2,1)} %bitcast.8, bf16[3,3,3,32,32]{4,3,2,1,0:T(8,128)(2,1)} %bitcast.5, f32[3,32]{1,0:T(4,128)} %bias_hbm.1, bf16[1,32]{1,0:T(2,128)(2,1)} %bitcast.9), custom_call_target="tpu_custom_call" | custom-call | tf_op jit(solution)/shard_map/contact/pallas_call | solution.py:301
  19.6 1.4 %copy.8 = f32[128,64]{0,1:T(8,128)} copy(f32[128,64]{0,1:T(8,128)} %bitcast.6) | data formatting | bytes 65536

commit v5 on v4

--- a/solution.py
+++ b/solution.py
@@ -124,14 +124,15 @@
             device_id_type=pl.DeviceIdType.MESH,
         )
 
+    def each_other(act):
+        for row in range(n):
+            pl.when(r != row)(lambda row=row: act(row))
+
     def broadcast(slot):
-        order = sorted(range(1, n), key=lambda k: -min(k, n - k))
-        for k in order:
-            copy(1, slot, (r + k) % n, 1 + k).start()
+        each_other(lambda row: copy(1, slot, row, 2 + row).start())
 
     def finish():
-        for k in range(1, n):
-            copy(1, 2, (r + k) % n, 1 + k).wait_send()
+        each_other(lambda row: copy(1, 2, row, 2 + row).wait_send())
 
     pl.when(is_owner)(lambda: broadcast(2))
     pl.when(is_side)(lambda: broadcast(3))
@@ -318,18 +319,25 @@
             pltpu.VMEM((ROWS, CH, LANES), jnp.bfloat16),
             pltpu.VMEM((ROWS, LANES), jnp.float32),
             pltpu.SemaphoreType.DMA((6,)),
-            pltpu.SemaphoreType.DMA((n + 1,)),
+            pltpu.SemaphoreType.DMA((n + 2,)),
             pltpu.SemaphoreType.DMA((4,)),
         ],
-        compiler_params=pltpu.CompilerParams(collective_id=0, has_side_effects=True),
+        compiler_params=pltpu.CompilerParams(
+            collective_id=0, has_side_effects=True, vmem_limit_bytes=16 * 2**20
+        ),
         name="contact",
     )(
-        embeddings,
-        row_weight.T,
-        col_weight.T,
-        conv_weights.transpose(0, 3, 4, 1, 2),
-        conv_bias,
-        head_weight.reshape(1, CH),
+        *[
+            pltpu.with_memory_space_constraint(each, pltpu.HBM)
+            for each in (
+                embeddings,
+                row_weight.T,
+                col_weight.T,
+                conv_weights.transpose(0, 3, 4, 1, 2),
+                conv_bias,
+                head_weight.reshape(1, CH),
+            )
+        ]
     )
     return contact.T
 

time: 21.1 us -> 19.5 us (0.924)
  the two profiles are of different devices: /device:TPU:27 before, /device:TPU:29 now
where the time goes in v5:
time: 19.5 us; the launch traced here: 19.4 us
  Pallas kernels  18.8 us (96%)
  local copies, waits for them, and re-layouts  0.62 us (3%)
    pallas_call x1, Pallas kernels, body(): pl.pallas_call(contact_kernel, out_shape=jax.ShapeDtypeStruct((COLS, ROWS...  18.8 us
    unnamed x1, local copies, waits for them, and re-layouts  0.62 us

profile of v5, /device:TPU:29, one launch (start us, length us, event | category | flops | bytes accessed | tf_op | source)
XLA Modules:
  0.0 19.4 jit_solution(5924392597178336142)
XLA Ops:
  0.0 18.8 %contact.1 = f32[64,128]{1,0:T(8,128)S(1)} custom-call(bf16[128,512]{1,0:T(8,128)(2,1)} %emb_hbm.1, bf16[32,512]{1,0:T(8,128)(2,1)} %bitcast.7, bf16[32,512]{1,0:T(8,128)(2,1)} %bitcast.8, bf16[3,3,3,32,32]{4,3,2,1,0:T(8,128)(2,1)} %bitcast.6, f32[3,32]{1,0:T(4,128)} %bias_hbm.1, bf16[1,32]{1,0:T(2,128)(2,1)} %bitcast.9), custom_call_target="tpu_custom_call" | custom-call | tf_op jit(solution)/shard_map/contact/pallas_call | solution.py:302
  18.8 0.6 %copy.8 = f32[128,64]{0,1:T(8,128)} copy(f32[128,64]{0,1:T(8,128)S(1)} %bitcast.5) | data formatting | bytes 65536

commit v6 on v5

--- a/solution.py
+++ b/solution.py
@@ -14,13 +14,14 @@
 GROUP = 6
 SPAN = GROUP + 2
 SIDE = 32
+PACKED = ROWS // 2
 DILATIONS = (1, 2, 4)
 
 
 def starts(level):
     dilation = DILATIONS[level]
     reach = sum(DILATIONS[: level + 1])
-    first, last = reach, TALL - reach
+    first, last = reach, (TALL - reach if level < 2 else reach + PACKED)
     found = []
     for phase in range(dilation):
         rows = list(range(first + phase, last, dilation))
@@ -51,6 +52,7 @@
     band,
     xa,
     xb,
+    xc,
     last,
     gathered,
     load_sem,
@@ -162,7 +164,7 @@
 
     f32, bf16 = jnp.float32, jnp.bfloat16
     lane = lax.broadcasted_iota(jnp.int32, (CH, LANES), 1)
-    column = lane + (c * COLS - SIDE)
+    column = lane + c * COLS - jnp.where(lane >= LANES - SIDE, LANES, 0)
     inside = jnp.logical_and(column >= 0, column < m * COLS)
     keep = jnp.where(inside, 1.0, 0.0)
     above = jnp.where(r > 0, 1.0, 0.0)
@@ -224,11 +226,11 @@
 
     col_own = land[2].astype(f32)
     col_side = land[3].astype(f32)
-    low = jnp.where(lane >= SIDE, pltpu.roll(col_own, SIDE, 1), pltpu.roll(col_side, SIDE, 1))
+    low = jnp.where(lane < LANES - SIDE, col_own, col_side)
     high = jnp.where(
-        lane < LANES - SIDE,
-        pltpu.roll(col_own, LANES - SIDE, 1),
-        pltpu.roll(col_side, LANES - SIDE, 1),
+        jnp.logical_and(lane >= COLS, lane < LANES - SIDE),
+        pltpu.roll(col_side, COLS, 1),
+        pltpu.roll(col_own, COLS, 1),
     )
     cols = [part.astype(bf16) for part in taps(jnp.where(half == 0, low, high), DILATIONS[0])]
     cols_kept = [cols[tap] * kept[1][tap] for tap in range(3)]
@@ -263,7 +265,18 @@
         gathered[at : at + SPAN] = lines[:, :LANES]
         gathered[at + SPAN : at + 2 * SPAN] = lines[:, LANES:]
 
-    refs = (xa, xb, xa)
+    def pack(row, piece):
+        for tap in range(3):
+            ahead = DILATIONS[2] * (tap - 1)
+            if row < HALO + PACKED + DILATIONS[2]:
+                moved = pltpu.roll(piece, (LANES - ahead) % LANES, 1) if ahead else piece
+                moved = moved.astype(bf16)
+                xc[tap, row, :, :COLS] = moved[:, :COLS]
+            if row >= HALO + PACKED - DILATIONS[2]:
+                moved = pltpu.roll(piece, COLS - ahead, 1).astype(bf16)
+                xc[tap, row - PACKED, :, COLS:] = moved[:, COLS:]
+
+    refs = (xa, xb, xc)
     for level, dilation in enumerate(DILATIONS):
         source = refs[level]
         begun = starts(level)
@@ -286,11 +299,16 @@
                     if level == 2:
                         last[row - HALO] = piece.astype(bf16)
                         continue
+                    if level == 1:
+                        pack(row, piece)
+                        continue
                     for tap, moved in enumerate(taps(piece, DILATIONS[level + 1])):
                         refs[level + 1][tap, row] = moved.astype(bf16)
-    for at in range(0, ROWS, 2 * SPAN):
+    for at in range(0, PACKED, 2 * SPAN):
         apply_head(at)
-    out_ref[...] = gathered[...].T[SIDE : SIDE + COLS]
+    turned = gathered[...].T
+    out_ref[:, :PACKED] = turned[:COLS]
+    out_ref[:, PACKED:] = turned[COLS:]
     pl.when(r > 0)(lambda: copy(0, 1, r - 1, 0).wait_send())
     pl.when(r < n - 1)(lambda: copy(0, 0, r + 1, 1).wait_send())
     pl.when(jnp.logical_or(is_owner, is_side))(finish)
@@ -316,8 +334,9 @@
             pltpu.VMEM((3, ROWS, CH, LANES), jnp.bfloat16),
             pltpu.VMEM((3, TALL, CH, LANES), jnp.bfloat16),
             pltpu.VMEM((3, TALL, CH, LANES), jnp.bfloat16),
-            pltpu.VMEM((ROWS, CH, LANES), jnp.bfloat16),
-            pltpu.VMEM((ROWS, LANES), jnp.float32),
+            pltpu.VMEM((3, HALO + PACKED + DILATIONS[2], CH, LANES), jnp.bfloat16),
+            pltpu.VMEM((PACKED, CH, LANES), jnp.bfloat16),
+            pltpu.VMEM((PACKED, LANES), jnp.float32),
             pltpu.SemaphoreType.DMA((6,)),
             pltpu.SemaphoreType.DMA((n + 2,)),
             pltpu.SemaphoreType.DMA((4,)),

time: 19.5 us -> 19.3 us (0.990)
  the two profiles are of different devices: /device:TPU:29 before, /device:TPU:37 now
where the time goes in v6:
time: 19.3 us; the launch traced here: 19.2 us
  Pallas kernels  18.6 us (96%)
  local copies, waits for them, and re-layouts  0.62 us (3%)
    pallas_call x1, Pallas kernels, body(): pl.pallas_call(contact_kernel, out_shape=jax.ShapeDtypeStruct((COLS, ROWS...  18.6 us
    unnamed x1, local copies, waits for them, and re-layouts  0.62 us

profile of v6, /device:TPU:37, one launch (start us, length us, event | category | flops | bytes accessed | tf_op | source)
XLA Modules:
  0.0 19.2 jit_solution(3562491618569440134)
XLA Ops:
  0.0 18.6 %contact.1 = f32[64,128]{1,0:T(8,128)S(1)} custom-call(bf16[128,512]{1,0:T(8,128)(2,1)} %emb_hbm.1, bf16[32,512]{1,0:T(8,128)(2,1)} %bitcast.7, bf16[32,512]{1,0:T(8,128)(2,1)} %bitcast.8, bf16[3,3,3,32,32]{4,3,2,1,0:T(8,128)(2,1)} %bitcast.6, f32[3,32]{1,0:T(4,128)} %bias_hbm.1, bf16[1,32]{1,0:T(2,128)(2,1)} %bitcast.9), custom_call_target="tpu_custom_call" | custom-call | tf_op jit(solution)/shard_map/contact/pallas_call | solution.py:320
  18.6 0.6 %copy.8 = f32[128,64]{0,1:T(8,128)} copy(f32[128,64]{0,1:T(8,128)S(1)} %bitcast.5) | data formatting | bytes 65536

commit v7 on v6

--- a/solution.py
+++ b/solution.py
@@ -85,6 +85,10 @@
     has_side = jnp.logical_and(side >= 0, side < n)
     is_owner = r == owner
     is_side = r == side
+    low_rows = n // 2
+    relay = jnp.where(c >= 2 * n - 3, n - 3, n - 1)
+    is_relay = r == relay
+    direct = jnp.logical_or(r < low_rows, is_relay)
     barrier = pltpu.get_barrier_semaphore()
 
     def greet(row):
@@ -94,8 +98,11 @@
 
     pl.when(r > 0)(lambda: greet(r - 1))
     pl.when(r < n - 1)(lambda: greet(r + 1))
-    pl.when(jnp.logical_not(is_owner))(lambda: greet(owner))
-    pl.when(jnp.logical_and(has_side, jnp.logical_not(is_side)))(lambda: greet(side))
+    pl.when(jnp.logical_and(direct, jnp.logical_not(is_owner)))(lambda: greet(owner))
+    pl.when(jnp.logical_and(jnp.logical_and(direct, has_side), jnp.logical_not(is_side)))(
+        lambda: greet(side)
+    )
+    pl.when(jnp.logical_not(direct))(lambda: greet(relay))
 
     for load in loads[:3]:
         load.wait()
@@ -111,8 +118,9 @@
     expected = (
         jnp.where(r > 0, 1, 0)
         + jnp.where(r < n - 1, 1, 0)
-        + jnp.where(is_owner, n - 1, 0)
-        + jnp.where(is_side, n - 1, 0)
+        + jnp.where(jnp.logical_or(is_owner, is_side), low_rows + 1, 0)
+        - jnp.where(jnp.logical_and(jnp.logical_or(is_owner, is_side), r < low_rows), 1, 0)
+        + jnp.where(is_relay, n - low_rows - 1, 0)
     )
     pl.semaphore_wait(barrier, expected)
 
@@ -126,15 +134,30 @@
             device_id_type=pl.DeviceIdType.MESH,
         )
 
-    def each_other(act):
-        for row in range(n):
+    def each_direct(act):
+        for row in range(low_rows):
             pl.when(r != row)(lambda row=row: act(row))
+        act(relay)
+
+    def each_high(source_row, act):
+        for row in range(low_rows, n):
+            pl.when(jnp.logical_and(row != relay, row != source_row))(lambda row=row: act(row))
 
     def broadcast(slot):
-        each_other(lambda row: copy(1, slot, row, 2 + row).start())
+        each_direct(lambda row: copy(1, slot, row, 2 + row).start())
 
     def finish():
-        each_other(lambda row: copy(1, 2, row, 2 + row).wait_send())
+        each_direct(lambda row: copy(1, 2, row, 2 + row).wait_send())
+
+    def forward(slot, row):
+        return pltpu.make_async_remote_copy(
+            src_ref=land.at[slot],
+            dst_ref=land.at[slot],
+            send_sem=send_sem.at[2 + row + (slot - 2) * n],
+            recv_sem=recv_sem.at[slot],
+            device_id=(row, c),
+            device_id_type=pl.DeviceIdType.MESH,
+        )
 
     pl.when(is_owner)(lambda: broadcast(2))
     pl.when(is_side)(lambda: broadcast(3))
@@ -222,6 +245,10 @@
     pl.when(jnp.logical_not(is_owner))(lambda: copy(1, 2, owner, 2).wait_recv())
     pl.when(jnp.logical_and(has_side, jnp.logical_not(is_side)))(
         lambda: copy(1, 3, side, 2).wait_recv()
+    )
+    pl.when(is_relay)(lambda: each_high(owner, lambda row: forward(2, row).start()))
+    pl.when(jnp.logical_and(is_relay, has_side))(
+        lambda: each_high(side, lambda row: forward(3, row).start())
     )
 
     col_own = land[2].astype(f32)
@@ -312,6 +339,10 @@
     pl.when(r > 0)(lambda: copy(0, 1, r - 1, 0).wait_send())
     pl.when(r < n - 1)(lambda: copy(0, 0, r + 1, 1).wait_send())
     pl.when(jnp.logical_or(is_owner, is_side))(finish)
+    pl.when(is_relay)(lambda: each_high(owner, lambda row: forward(2, row).wait_send()))
+    pl.when(jnp.logical_and(is_relay, has_side))(
+        lambda: each_high(side, lambda row: forward(3, row).wait_send())
+    )
 
 
 def body(embeddings, row_weight, col_weight, conv_weights, conv_bias, head_weight):
@@ -338,7 +369,7 @@
             pltpu.VMEM((PACKED, CH, LANES), jnp.bfloat16),
             pltpu.VMEM((PACKED, LANES), jnp.float32),
             pltpu.SemaphoreType.DMA((6,)),
-            pltpu.SemaphoreType.DMA((n + 2,)),
+            pltpu.SemaphoreType.DMA((2 * n + 2,)),
             pltpu.SemaphoreType.DMA((4,)),
         ],
         compiler_params=pltpu.CompilerParams(

time: 19.3 us -> 18.9 us (0.979)
  the two profiles are of different devices: /device:TPU:37 before, /device:TPU:27 now
where the time goes in v7:
time: 18.9 us; the launch traced here: 18.8 us
  Pallas kernels  18.1 us (96%)
  local copies, waits for them, and re-layouts  0.62 us (3%)
    pallas_call x1, Pallas kernels, body(): pl.pallas_call(contact_kernel, out_shape=jax.ShapeDtypeStruct((COLS, ROWS...  18.1 us
    unnamed x1, local copies, waits for them, and re-layouts  0.62 us

profile of v7, /device:TPU:27, one launch (start us, length us, event | category | flops | bytes accessed | tf_op | source)
XLA Modules:
  0.0 18.8 jit_solution(5607892949907446928)
XLA Ops:
  0.0 18.1 %contact.1 = f32[64,128]{1,0:T(8,128)S(1)} custom-call(bf16[128,512]{1,0:T(8,128)(2,1)} %emb_hbm.1, bf16[32,512]{1,0:T(8,128)(2,1)} %bitcast.7, bf16[32,512]{1,0:T(8,128)(2,1)} %bitcast.8, bf16[3,3,3,32,32]{4,3,2,1,0:T(8,128)(2,1)} %bitcast.6, f32[3,32]{1,0:T(4,128)} %bias_hbm.1, bf16[1,32]{1,0:T(2,128)(2,1)} %bitcast.9), custom_call_target="tpu_custom_call" | custom-call | tf_op jit(solution)/shard_map/contact/pallas_call | solution.py:351
  18.1 0.6 %copy.8 = f32[128,64]{0,1:T(8,128)} copy(f32[128,64]{0,1:T(8,128)S(1)} %bitcast.5) | data formatting | bytes 65536

commit v8 on v7

--- a/solution.py
+++ b/solution.py
@@ -86,7 +86,8 @@
     is_owner = r == owner
     is_side = r == side
     low_rows = n // 2
-    relay = jnp.where(c >= 2 * n - 3, n - 3, n - 1)
+    taken = jnp.logical_and(c >= n - 1, c <= n + 2)
+    relay = jnp.where(taken, low_rows + 2, low_rows)
     is_relay = r == relay
     direct = jnp.logical_or(r < low_rows, is_relay)
     barrier = pltpu.get_barrier_semaphore()

time: 18.9 us -> 17.6 us (0.931)
  the two profiles are of different devices: /device:TPU:27 before, /device:TPU:37 now
where the time goes in v8:
time: 17.6 us; the launch traced here: 17.5 us
  Pallas kernels  16.8 us (95%)
  local copies, waits for them, and re-layouts  0.62 us (4%)
    pallas_call x1, Pallas kernels, body(): pl.pallas_call(contact_kernel, out_shape=jax.ShapeDtypeStruct((COLS, ROWS...  16.8 us
    unnamed x1, local copies, waits for them, and re-layouts  0.62 us

profile of v8, /device:TPU:37, one launch (start us, length us, event | category | flops | bytes accessed | tf_op | source)
XLA Modules:
  0.0 17.5 jit_solution(3383175878888336722)
XLA Ops:
  0.0 16.8 %contact.1 = f32[64,128]{1,0:T(8,128)S(1)} custom-call(bf16[128,512]{1,0:T(8,128)(2,1)} %emb_hbm.1, bf16[32,512]{1,0:T(8,128)(2,1)} %bitcast.7, bf16[32,512]{1,0:T(8,128)(2,1)} %bitcast.8, bf16[3,3,3,32,32]{4,3,2,1,0:T(8,128)(2,1)} %bitcast.6, f32[3,32]{1,0:T(4,128)} %bias_hbm.1, bf16[1,32]{1,0:T(2,128)(2,1)} %bitcast.9), custom_call_target="tpu_custom_call" | custom-call | tf_op jit(solution)/shard_map/contact/pallas_call | solution.py:352
  16.8 0.6 %copy.8 = f32[128,64]{0,1:T(8,128)} copy(f32[128,64]{0,1:T(8,128)S(1)} %bitcast.5) | data formatting | bytes 65536
